TPU v7x, 32 devices: a whole 2x2x4 slice. The times are simulated.
32 devices in a mesh: fsdp: 8 (over z, core), ctx: 2 (over x), tp: 2 (over y).
Axes of the slice: x: 2, y: 2, z: 4, core: 2. Of those that a mesh axis runs over, the one named last changes fastest.
Arguments:
- block_input: bfloat16 [8, 384, 1024], P('fsdp', 'ctx'), may hold values from -6 to 6
- segments: int32 [8, 384], P('fsdp', 'ctx'), may hold values from 0 to 3, never falling along the last dimension, each value on 1 to 192 neighbouring positions
- norm1_gain: bfloat16 [1024], P('fsdp'), may hold values from 0.5 to 1.5
- q_weight: bfloat16 [1024, 1024], P('fsdp', 'tp'), may hold values from -0.1875 to 0.1875
- k_weight: bfloat16 [1024, 1024], P('fsdp', 'tp'), may hold values from -0.1875 to 0.1875
- v_weight: bfloat16 [1024, 2048], P('fsdp', 'tp'), may hold values from -0.1875 to 0.1875
- decay_weight: bfloat16 [1024, 8], P('fsdp', 'tp'), may hold values from -0.1875 to 0.1875
- beta_weight: bfloat16 [1024, 8], P('fsdp', 'tp'), may hold values from -0.1875 to 0.1875
- gate_weight: bfloat16 [1024, 2048], P('fsdp', 'tp'), may hold values from -0.1875 to 0.1875
- conv_weight: bfloat16 [4096, 4], P(('tp', 'fsdp')), may hold values from -3 to 3
- decay_rate: float32 [8], P('tp'), may hold values from 0.0005 to 0.05
- head_gain: bfloat16 [256], P('fsdp'), may hold values from 0.5 to 1.5
- out_weight: bfloat16 [1024, 2048], P('fsdp', 'tp'), may hold values from -0.25 to 0.25
- norm2_gain: bfloat16 [1024], P('fsdp'), may hold values from 0.5 to 1.5
- ffn_gate: bfloat16 [1024, 2816], P('fsdp', 'tp'), may hold values from -0.1875 to 0.1875
- ffn_up: bfloat16 [1024, 2816], P('fsdp', 'tp'), may hold values from -0.1875 to 0.1875
- ffn_down: bfloat16 [1024, 2816], P('fsdp', 'tp'), may hold values from -0.109375 to 0.109375
- cotangent: bfloat16 [8, 384, 1024], P('fsdp', 'ctx'), may hold values from -6 to 6
Outputs:
- block_output: bfloat16 [8, 384, 1024], P('fsdp', 'ctx')
- input_grad: float32 [8, 384, 1024], P('fsdp', 'ctx')
- norm1_gain_grad: float32 [1024], P('fsdp')
- q_weight_grad: float32 [1024, 1024], P('fsdp', 'tp')
- k_weight_grad: float32 [1024, 1024], P('fsdp', 'tp')
- v_weight_grad: float32 [1024, 2048], P('fsdp', 'tp')
- decay_weight_grad: float32 [1024, 8], P('fsdp', 'tp')
- beta_weight_grad: float32 [1024, 8], P('fsdp', 'tp')
- gate_weight_grad: float32 [1024, 2048], P('fsdp', 'tp')
- conv_weight_grad: float32 [4096, 4], P(('tp', 'fsdp'))
- decay_rate_grad: float32 [8], P('tp')
- head_gain_grad: float32 [256], P('fsdp')
- out_weight_grad: float32 [1024, 2048], P('fsdp', 'tp')
- norm2_gain_grad: float32 [1024], P('fsdp')
- ffn_gate_grad: float32 [1024, 2816], P('fsdp', 'tp')
- ffn_up_grad: float32 [1024, 2816], P('fsdp', 'tp')
- ffn_down_grad: float32 [1024, 2816], P('fsdp', 'tp')
Inputs may be any that keep to these rules, and one draw needn't show every extreme that they name: `segments`: segment numbers never fall along a sequence; a document has 1 to 192 tokens and one document of each sequence has exactly 192.
All inputs are finite; a program needn't handle non-finite values.
Results may differ from a plain program's by a relative error of at most 0.014.
Values may be sent and summed in bfloat16 or wider, within the bound.
A program may use at most 192 MiB of HBM per device.

v0:
```python
import jax
import jax.numpy as jnp
from jax import lax
from jax.sharding import PartitionSpec as P

DK = 128
DV = 256
GROUP = 64


EPSILON = 1e-06
HIGHEST = lax.Precision.HIGHEST


def shifted(block, axis, distance):
    devices = range(lax.axis_size(axis))
    route = [(i - distance, i) for i in devices if i - distance in devices]
    return lax.ppermute(block, axis, route)


def rms_scale(values, gain_vec):
    return (
        values * lax.rsqrt(jnp.mean(values * values, axis=-1, keepdims=True) + EPSILON) * gain_vec
    )


def unit_length(values):
    return values * lax.rsqrt(jnp.sum(values * values, axis=-1, keepdims=True) + EPSILON)


def swiglu(gate_in, up_in):
    return jax.nn.silu(gate_in) * up_in


def assemble(query_pre, key_pre, value_pre, head_count):
    length = query_pre.shape[0]
    joined = jnp.concatenate(
        [
            query_pre.reshape(length, head_count, -1),
            key_pre.reshape(length, head_count, -1),
            value_pre.reshape(length, head_count, -1),
        ],
        axis=2,
    )
    return joined.reshape(length, -1)


def conv_front(mixed_pre, decay_pre, beta_pre, edge_pre, conv_taps, rate_vec, seg_value, edge_seg):
    taps_count = conv_taps.shape[1]
    length = mixed_pre.shape[0]
    head_count = decay_pre.shape[1]
    extended = jnp.concatenate([edge_pre, mixed_pre], axis=0)
    seg_ext = jnp.concatenate([edge_seg, seg_value], axis=0)
    mixed_sum = jnp.zeros_like(mixed_pre)
    for shift_back in range(taps_count):
        offset = taps_count - 1 - shift_back
        window = extended[offset : offset + length]
        same_doc = (seg_ext[offset : offset + length] == seg_value).astype(jnp.float32)
        mixed_sum = mixed_sum + conv_taps[:, shift_back] * window * same_doc[:, None]
    activated = jax.nn.silu(mixed_sum).reshape(length, head_count, -1)
    query_vec = unit_length(activated[:, :, :DK]) * DK ** (-0.5)
    key_vec = unit_length(activated[:, :, DK : 2 * DK])
    value_vec = activated[:, :, 2 * DK :]
    beta_gate = jax.nn.sigmoid(beta_pre)
    log_decay = -rate_vec * jax.nn.softplus(decay_pre)
    return (query_vec, key_vec, value_vec, beta_gate, log_decay)


def split_blocks(array):
    blocks = array.shape[0] // GROUP
    shaped = array.reshape((blocks, GROUP) + array.shape[1:])
    return jnp.moveaxis(shaped, 2, 0)


def group_prep(query_vec, key_vec, value_vec, beta_gate, log_decay, seg_value, seg_before):
    query_blk = split_blocks(query_vec)
    key_blk = split_blocks(key_vec)
    value_blk = split_blocks(value_vec)
    beta_blk = split_blocks(beta_gate)
    decay_cum = jnp.cumsum(split_blocks(log_decay), axis=-1)
    seg_blk = seg_value.reshape(-1, GROUP)
    same_doc = seg_blk[:, :, None] == seg_blk[:, None, :]
    row_ids = lax.broadcasted_iota(jnp.int32, (GROUP, GROUP), 0)
    col_ids = lax.broadcasted_iota(jnp.int32, (GROUP, GROUP), 1)
    lower_mask = (row_ids >= col_ids) & same_doc
    strict = (row_ids > col_ids) & same_doc
    log_gap = decay_cum[..., :, None] - decay_cum[..., None, :]
    decay_pair = jnp.where(lower_mask, jnp.exp(jnp.where(lower_mask, log_gap, 0.0)), 0.0)
    decay_strict = jnp.where(strict, decay_pair, 0.0)
    from_start = jnp.where(seg_blk == seg_before[:, None], jnp.exp(decay_cum), 0.0)
    last_cum = decay_cum[..., -1:]
    to_end = jnp.where(seg_blk == seg_blk[:, -1:], jnp.exp(last_cum - decay_cum), 0.0)
    keep_whole = jnp.where(seg_blk[:, -1] == seg_before, jnp.exp(last_cum[..., 0]), 0.0)
    key_gram = jnp.einsum("hncd,hnjd->hncj", key_blk, key_blk, precision=HIGHEST)
    system = jnp.eye(GROUP, dtype=jnp.float32) + key_gram * decay_strict * beta_blk[..., :, None]
    wide_keys = lax.linalg.triangular_solve(
        system,
        (beta_blk * from_start)[..., None] * key_blk,
        left_side=True,
        lower=True,
        unit_diagonal=True,
    )
    new_values = lax.linalg.triangular_solve(
        system, beta_blk[..., None] * value_blk, left_side=True, lower=True, unit_diagonal=True
    )
    scores = jnp.einsum("hncd,hnjd->hncj", query_blk, key_blk, precision=HIGHEST) * decay_pair
    query_dec = query_blk * from_start[..., None]
    key_dec = key_blk * to_end[..., None]
    return (wide_keys, new_values, scores, query_dec, key_dec, keep_whole)


def group_run(prepared, state_start):
    items = tuple((jnp.moveaxis(array, 1, 0) for array in prepared))

    def advance(state_now, block_items):
        wide_keys, new_values, scores, query_dec, key_dec, keep_whole = block_items
        fresh = new_values - jnp.einsum("hcd,hde->hce", wide_keys, state_now, precision=HIGHEST)
        result = jnp.einsum("hcd,hde->hce", query_dec, state_now, precision=HIGHEST) + jnp.einsum(
            "hcj,hje->hce", scores, fresh, precision=HIGHEST
        )
        state_next = keep_whole[:, None, None] * state_now + jnp.einsum(
            "hcd,hce->hde", key_dec, fresh, precision=HIGHEST
        )
        return (state_next, result)

    state_end, results = lax.scan(advance, state_start, items)
    blocks, head_count, width_c, width_v = results.shape
    return (
        jnp.transpose(results, (0, 2, 1, 3)).reshape(blocks * width_c, head_count, width_v),
        state_end,
    )


def group_states(prepared, state_start):
    wide_keys, new_values, _, _, key_dec, keep_whole = prepared
    items = tuple(
        (jnp.moveaxis(array, 1, 0) for array in (wide_keys, new_values, key_dec, keep_whole))
    )

    def advance(state_now, block_items):
        wide_blk, value_blk, key_blk, keep_blk = block_items
        fresh = value_blk - jnp.einsum("hcd,hde->hce", wide_blk, state_now, precision=HIGHEST)
        return (
            keep_blk[:, None, None] * state_now
            + jnp.einsum("hcd,hce->hde", key_blk, fresh, precision=HIGHEST),
            None,
        )

    state_end, _ = lax.scan(advance, state_start, items)
    return state_end


def start_grad(prepared, d_outputs, grad_zero):
    wide_keys, _, scores, query_dec, key_dec, keep_whole = prepared
    d_blocks = split_blocks(d_outputs)
    items = tuple(
        (
            jnp.moveaxis(array, 1, 0)
            for array in (wide_keys, scores, query_dec, key_dec, keep_whole, d_blocks)
        )
    )

    def retreat(grad_next, block_items):
        wide_blk, score_blk, query_blk, key_blk, keep_blk, d_blk = block_items
        d_fresh = jnp.einsum("hcj,hce->hje", score_blk, d_blk, precision=HIGHEST) + jnp.einsum(
            "hcd,hde->hce", key_blk, grad_next, precision=HIGHEST
        )
        grad_now = (
            keep_blk[:, None, None] * grad_next
            + jnp.einsum("hcd,hce->hde", query_blk, d_blk, precision=HIGHEST)
            - jnp.einsum("hcd,hce->hde", wide_blk, d_fresh, precision=HIGHEST)
        )
        return (grad_now, None)

    grad_start, _ = lax.scan(retreat, grad_zero, items, reverse=True)
    return grad_start


def group_map(prepared):
    wide_keys, _, _, _, key_dec, keep_whole = prepared
    unit_mat = jnp.eye(wide_keys.shape[-1], dtype=jnp.float32)
    transitions = keep_whole[..., None, None] * unit_mat - jnp.einsum(
        "hncd,hnce->hnde", key_dec, wide_keys, precision=HIGHEST
    )

    def advance(total, piece):
        return (jnp.einsum("hde,hef->hdf", piece, total, precision=HIGHEST), None)

    start = jnp.broadcast_to(unit_mat, (transitions.shape[0],) + unit_mat.shape)
    total, _ = lax.scan(advance, start, jnp.moveaxis(transitions, 1, 0))
    return total


def mixer_core(
    mixed_pre, decay_pre, beta_pre, edge_pre, conv_taps, rate_vec, state_start, seg_value, edge_seg
):
    query_vec, key_vec, value_vec, beta_gate, log_decay = conv_front(
        mixed_pre, decay_pre, beta_pre, edge_pre, conv_taps, rate_vec, seg_value, edge_seg
    )
    seg_before = jnp.concatenate([edge_seg[-1:], seg_value[GROUP - 1 :: GROUP][:-1]])
    prepared = group_prep(
        query_vec, key_vec, value_vec, beta_gate, log_decay, seg_value, seg_before
    )
    return group_run(prepared, state_start)


def head_gate(outputs, gate_pre, gain_vec):
    normed = rms_scale(outputs, gain_vec)
    return (normed * jax.nn.silu(gate_pre.reshape(outputs.shape))).reshape(outputs.shape[0], -1)


def per_device(
    block_input,
    segments,
    norm1_gain,
    q_weight,
    k_weight,
    v_weight,
    decay_weight,
    beta_weight,
    gate_weight,
    conv_weight,
    decay_rate,
    head_gain,
    out_weight,
    norm2_gain,
    ffn_gate,
    ffn_up,
    ffn_down,
    cotangent,
):
    shards = (
        norm1_gain,
        q_weight,
        k_weight,
        v_weight,
        decay_weight,
        beta_weight,
        gate_weight,
        conv_weight,
        head_gain,
        out_weight,
        norm2_gain,
        ffn_gate,
        ffn_up,
        ffn_down,
    )
    whole = (
        lax.all_gather(shards[0], "fsdp", axis=0, tiled=True),
        lax.all_gather(shards[1], "fsdp", axis=0, tiled=True),
        lax.all_gather(shards[2], "fsdp", axis=0, tiled=True),
        lax.all_gather(shards[3], "fsdp", axis=0, tiled=True),
        lax.all_gather(shards[4], "fsdp", axis=0, tiled=True),
        lax.all_gather(shards[5], "fsdp", axis=0, tiled=True),
        lax.all_gather(shards[6], "fsdp", axis=0, tiled=True),
        lax.all_gather(shards[7], "fsdp", axis=0, tiled=True),
        lax.all_gather(shards[8], "fsdp", axis=0, tiled=True),
        lax.all_gather(shards[9], "fsdp", axis=0, tiled=True),
        lax.all_gather(shards[10], "fsdp", axis=0, tiled=True),
        lax.all_gather(shards[11], "fsdp", axis=0, tiled=True),
        lax.all_gather(shards[12], "fsdp", axis=0, tiled=True),
        lax.all_gather(shards[13], "fsdp", axis=0, tiled=True),
    )
    (
        gain_one,
        q_mat,
        k_mat,
        v_mat,
        decay_mat,
        beta_mat,
        gate_mat,
        conv_taps,
        gain_head,
        out_mat,
        gain_two,
        gate_ffn_mat,
        up_ffn_mat,
        down_ffn_mat,
    ) = whole
    row_input = block_input[0]
    seg_value = segments[0].astype(jnp.float32)
    row_cot = cotangent[0]
    length = row_input.shape[0]
    head_count = decay_mat.shape[1]
    taps_count = conv_taps.shape[1]
    tail_start = length - taps_count + 1
    input_wide = row_input.astype(jnp.float32)
    norm_one, norm_one_back = jax.vjp(rms_scale, input_wide, gain_one.astype(jnp.float32))
    normed_one = norm_one.astype(jnp.bfloat16)
    projected = [
        jnp.dot(normed_one, matrix, preferred_element_type=jnp.float32)
        for matrix in (q_mat, k_mat, v_mat, decay_mat, beta_mat, gate_mat)
    ]
    query_pre, key_pre, value_pre, decay_pre, beta_pre, gate_pre = projected
    mixed_pre = assemble(query_pre, key_pre, value_pre, head_count)
    edge_pre, edge_seg = shifted((mixed_pre[tail_start:], seg_value[tail_start:]), "ctx", 1)
    taps_wide = conv_taps.astype(jnp.float32)
    query_vec, key_vec, value_vec, beta_gate, log_decay = conv_front(
        mixed_pre, decay_pre, beta_pre, edge_pre, taps_wide, decay_rate, seg_value, edge_seg
    )
    seg_before = jnp.concatenate([edge_seg[-1:], seg_value[GROUP - 1 :: GROUP][:-1]])
    prepared = group_prep(
        query_vec, key_vec, value_vec, beta_gate, log_decay, seg_value, seg_before
    )
    state_zero = jnp.zeros((head_count, DK, DV), jnp.float32)
    carried = group_states(prepared, state_zero)
    moved = group_map(prepared)

    def forward_step(step_index, state_in):
        return shifted(
            (jnp.einsum("hde,hef->hdf", moved, state_in, precision=HIGHEST) + carried).astype(
                jnp.bfloat16
            ),
            "ctx",
            1,
        ).astype(jnp.float32)

    state_start = lax.fori_loop(0, lax.axis_size("ctx") - 1, forward_step, state_zero)
    outputs, _ = group_run(prepared, state_start)
    gated, gate_back = jax.vjp(head_gate, outputs, gate_pre, gain_head.astype(jnp.float32))
    gated_half = gated.astype(jnp.bfloat16)
    mixer_out = lax.psum(jnp.dot(gated_half, out_mat.T, preferred_element_type=jnp.float32), "tp")
    hidden = input_wide + mixer_out
    norm_two, norm_two_back = jax.vjp(rms_scale, hidden, gain_two.astype(jnp.float32))
    normed_two = norm_two.astype(jnp.bfloat16)
    gate_ffn = jnp.dot(normed_two, gate_ffn_mat, preferred_element_type=jnp.float32)
    up_ffn = jnp.dot(normed_two, up_ffn_mat, preferred_element_type=jnp.float32)
    product, swiglu_back = jax.vjp(swiglu, gate_ffn, up_ffn)
    hidden_units = product.astype(jnp.bfloat16)
    ffn_out = lax.psum(
        jnp.dot(hidden_units, down_ffn_mat.T, preferred_element_type=jnp.float32).astype(
            jnp.bfloat16
        ),
        "tp",
    ).astype(jnp.float32)
    block_out = (hidden + ffn_out).astype(jnp.bfloat16)
    d_units = jnp.dot(row_cot, down_ffn_mat, preferred_element_type=jnp.float32)
    g_down = jnp.dot(row_cot.T, hidden_units, preferred_element_type=jnp.float32)
    d_gate_ffn, d_up_ffn = swiglu_back(d_units)
    d_gate_half = d_gate_ffn.astype(jnp.bfloat16)
    d_up_half = d_up_ffn.astype(jnp.bfloat16)
    d_normed_part = jnp.dot(
        d_gate_half, gate_ffn_mat.T, preferred_element_type=jnp.float32
    ) + jnp.dot(d_up_half, up_ffn_mat.T, preferred_element_type=jnp.float32)
    d_normed_two = lax.psum(d_normed_part, "tp")
    g_gate_ffn = jnp.dot(normed_two.T, d_gate_half, preferred_element_type=jnp.float32)
    g_up_ffn = jnp.dot(normed_two.T, d_up_half, preferred_element_type=jnp.float32)
    d_hidden_two, g_gain_two = norm_two_back(d_normed_two)
    d_hidden = row_cot.astype(jnp.float32) + d_hidden_two
    d_hidden_half = d_hidden.astype(jnp.bfloat16)
    d_gated = jnp.dot(d_hidden_half, out_mat, preferred_element_type=jnp.float32)
    g_out = jnp.dot(d_hidden_half.T, gated_half, preferred_element_type=jnp.float32)
    d_outputs, d_gate_pre, g_head_part = gate_back(d_gated)
    local_start = start_grad(prepared, d_outputs, state_zero)
    transposed = jnp.swapaxes(moved, 1, 2)

    def backward_step(step_index, grad_after):
        return shifted(
            (
                jnp.einsum("hde,hef->hdf", transposed, grad_after, precision=HIGHEST) + local_start
            ).astype(jnp.bfloat16),
            "ctx",
            -1,
        ).astype(jnp.float32)

    state_grad = lax.fori_loop(0, lax.axis_size("ctx") - 1, backward_step, state_zero)

    def core_local(mixed_in, decay_in, beta_in, edge_in, taps_in, rate_in, state_in):
        return mixer_core(
            mixed_in, decay_in, beta_in, edge_in, taps_in, rate_in, state_in, seg_value, edge_seg
        )

    _, core_back = jax.vjp(
        core_local, mixed_pre, decay_pre, beta_pre, edge_pre, taps_wide, decay_rate, state_start
    )
    core_grads = core_back((d_outputs, state_grad))
    edge_grad = shifted(core_grads[3], "ctx", -1)
    d_mixed = core_grads[0] + jnp.pad(edge_grad, ((tail_start, 0), (0, 0)))
    d_split = d_mixed.reshape(length, head_count, -1)
    d_query = d_split[:, :, :DK].reshape(length, -1)
    d_key = d_split[:, :, DK : 2 * DK].reshape(length, -1)
    d_value = d_split[:, :, 2 * DK :].reshape(length, -1)
    halves = [
        item.astype(jnp.bfloat16)
        for item in (d_query, d_key, d_value, core_grads[1], core_grads[2], d_gate_pre)
    ]
    matrices = (q_mat, k_mat, v_mat, decay_mat, beta_mat, gate_mat)
    d_first_part = jnp.zeros_like(input_wide)
    for half_item, matrix in zip(halves, matrices):
        d_first_part = d_first_part + jnp.dot(
            half_item, matrix.T, preferred_element_type=jnp.float32
        )
    weight_grads = [
        jnp.dot(normed_one.T, half_item, preferred_element_type=jnp.float32) for half_item in halves
    ]
    d_normed_one, g_head = (
        lax.psum(d_first_part.astype(jnp.bfloat16), "tp").astype(jnp.float32),
        lax.psum(g_head_part.astype(jnp.bfloat16), "tp").astype(jnp.float32),
    )
    d_input_one, g_gain_one = norm_one_back(d_normed_one)
    input_grad = d_hidden + d_input_one
    rate_rows = jnp.broadcast_to(core_grads[5], (lax.axis_size("fsdp"), head_count))
    local_grads = (
        g_gain_one,
        weight_grads[0],
        weight_grads[1],
        weight_grads[2],
        weight_grads[3],
        weight_grads[4],
        weight_grads[5],
        core_grads[4],
        g_head,
        g_out,
        g_gain_two,
        g_gate_ffn,
        g_up_ffn,
        g_down,
        rate_rows,
    )
    shard_grads = (
        lax.psum_scatter(local_grads[0], "fsdp", scatter_dimension=0, tiled=True),
        lax.psum_scatter(local_grads[1], "fsdp", scatter_dimension=0, tiled=True),
        lax.psum_scatter(local_grads[2], "fsdp", scatter_dimension=0, tiled=True),
        lax.psum_scatter(local_grads[3], "fsdp", scatter_dimension=0, tiled=True),
        lax.psum_scatter(local_grads[4], "fsdp", scatter_dimension=0, tiled=True),
        lax.psum_scatter(local_grads[5], "fsdp", scatter_dimension=0, tiled=True),
        lax.psum_scatter(local_grads[6], "fsdp", scatter_dimension=0, tiled=True),
        lax.psum_scatter(local_grads[7], "fsdp", scatter_dimension=0, tiled=True),
        lax.psum_scatter(local_grads[8], "fsdp", scatter_dimension=0, tiled=True),
        lax.psum_scatter(local_grads[9], "fsdp", scatter_dimension=0, tiled=True),
        lax.psum_scatter(local_grads[10], "fsdp", scatter_dimension=0, tiled=True),
        lax.psum_scatter(local_grads[11], "fsdp", scatter_dimension=0, tiled=True),
        lax.psum_scatter(local_grads[12], "fsdp", scatter_dimension=0, tiled=True),
        lax.psum_scatter(local_grads[13], "fsdp", scatter_dimension=0, tiled=True),
        lax.psum_scatter(local_grads[14], "fsdp", scatter_dimension=0, tiled=True),
    )
    summed = (
        lax.psum(shard_grads[0].astype(jnp.bfloat16), "ctx").astype(jnp.float32),
        lax.psum(shard_grads[1].astype(jnp.bfloat16), "ctx").astype(jnp.float32),
        lax.psum(shard_grads[2].astype(jnp.bfloat16), "ctx").astype(jnp.float32),
        lax.psum(shard_grads[3].astype(jnp.bfloat16), "ctx").astype(jnp.float32),
        lax.psum(shard_grads[4].astype(jnp.bfloat16), "ctx").astype(jnp.float32),
        lax.psum(shard_grads[5].astype(jnp.bfloat16), "ctx").astype(jnp.float32),
        lax.psum(shard_grads[6].astype(jnp.bfloat16), "ctx").astype(jnp.float32),
        lax.psum(shard_grads[7].astype(jnp.bfloat16), "ctx").astype(jnp.float32),
        lax.psum(shard_grads[8].astype(jnp.bfloat16), "ctx").astype(jnp.float32),
        lax.psum(shard_grads[9].astype(jnp.bfloat16), "ctx").astype(jnp.float32),
        lax.psum(shard_grads[10].astype(jnp.bfloat16), "ctx").astype(jnp.float32),
        lax.psum(shard_grads[11].astype(jnp.bfloat16), "ctx").astype(jnp.float32),
        lax.psum(shard_grads[12].astype(jnp.bfloat16), "ctx").astype(jnp.float32),
        lax.psum(shard_grads[13].astype(jnp.bfloat16), "ctx").astype(jnp.float32),
        lax.psum(shard_grads[14].astype(jnp.bfloat16), "ctx").astype(jnp.float32),
    )
    return (
        block_out[None],
        input_grad[None],
        summed[0],
        summed[1],
        summed[2],
        summed[3],
        summed[4],
        summed[5],
        summed[6],
        summed[7],
        summed[14][0],
        summed[8],
        summed[9],
        summed[10],
        summed[11],
        summed[12],
        summed[13],
    )


def solution(mesh):
    placed = (
        P("fsdp", "ctx", None),
        P("fsdp", "ctx"),
        P("fsdp"),
        P("fsdp", "tp"),
        P("fsdp", "tp"),
        P("fsdp", "tp"),
        P("fsdp", "tp"),
        P("fsdp", "tp"),
        P("fsdp", "tp"),
        P(("tp", "fsdp"), None),
        P("tp"),
        P("fsdp"),
        P("fsdp", "tp"),
        P("fsdp"),
        P("fsdp", "tp"),
        P("fsdp", "tp"),
        P("fsdp", "tp"),
        P("fsdp", "ctx", None),
    )
    return jax.shard_map(
        per_device,
        mesh=mesh,
        in_specs=placed,
        out_specs=(
            P("fsdp", "ctx", None),
            P("fsdp", "ctx", None),
            P("fsdp"),
            P("fsdp", "tp"),
            P("fsdp", "tp"),
            P("fsdp", "tp"),
            P("fsdp", "tp"),
            P("fsdp", "tp"),
            P("fsdp", "tp"),
            P(("tp", "fsdp"), None),
            P("tp"),
            P("fsdp"),
            P("fsdp", "tp"),
            P("fsdp"),
            P("fsdp", "tp"),
            P("fsdp", "tp"),
            P("fsdp", "tp"),
        ),
        check_vma=False,
    )
```

profile of v0, /device:TPU:0, one launch (start us, length us, event | category | flops | bytes accessed | tf_op | source)
XLA Modules:
  0.0 1193.0 jit_solution(17037708100920461702)
XLA Ops:
  10.8 4.9 collective-permute-start
  20.0 16.6 %all-reduce.13 = bf16[256]{0:T(256)(128)(2,1)S(1)} all-reduce(bf16[256]{0:T(256)(128)(2,1)S(1)} %dynamic-update-slice), channel_id=1, replica_groups=mesh['fsdp'=8,'ctx'=2,'tp'=2] {'fsdp'}, use_global_device_ids=true, to_apply=%add.13 | all-reduce | flops 256 | bytes 1024
  37.8 8.7 all_gather.43
  46.6 10.5 all-gather
  60.7 12.8 %all_gather.44 = bf16[2048,4]{0,1:T(4,128)(2,1)S(1)} all-gather(bf16[256,4]{0,1:T(4,128)(2,1)S(1)} %copy-done.142), channel_id=1, replica_groups=mesh['fsdp'=8,'ctx'=2,'tp'=2] {'fsdp'}, dimensions={0}, use_global_device_ids=true | all-gather | bytes 18432 | tf_op jit(solution)/shard_map/all_gather | solution.py:256
  73.5 9.1 all_gather.48
  92.8 3.9 copy.332
  102.3 16.6 %all-gather.17.cloned.1.call-done = bf16[1024,1024]{1,0:T(8,128)(2,1)} async-done(((bf16[128,1024]{1,0:T(8,128)(2,1)}), bf16[1024,1024]{1,0:T(8,128)(2,1)}) %all-gather.17.cloned.1.call-update) | async-done | bytes 2097168 | tf_op jit(solution)/shard_map/all_gather | solution.py:255
  118.9 3.9 copy.359
  122.8 3.5 fusion.171
  140.5 59.0 %custom-call.18 = f32[4,3,1,64,64]{3,4,2,1,0:T(8,128)S(1)} custom-call(f32[4,3,1,64,64]{4,3,2,1,0:T(8,128)S(1)} %add_bitcast_fusion), custom_call_target="InvertDiagBlocksLowerTriangular" | custom-call | tf_op jit(solution)/shard_map/triangular_solve/custom-call.1 | solution.py:96
  201.6 5.6 while.102
  209.7 4.2 while.98
  214.4 3.6 collective-permute-start.2
  224.7 15.5 %while.99 = (s32[]{:T(128)}, f32[4,128,256]{2,1,0:T(8,128)S(1)}, f32[3,4,64,256]{3,2,1,0:T(8,128)}, f32[3,4]{1,0:T(4,128)}, f32[3,4,64,128]{3,2,1,0:T(8,128)S(1)...) while((s32[]{:T(128)}, f32[4,128,256]{2,1,0:T(8,128)S(1)}, ...), condition=%wide.region_9.12_spmd, body=%wide.region_8.11_spmd.sunk | while | flops 352714752 | bytes 4459161 | solution.py:126
  244.6 3.4 fusion.289
  250.3 10.3 all-gather.1
  260.6 22.5 %all-reduce.27.cloned.1.call-done = f32[192,1024]{1,0:T(8,128)} async-done(((f32[192,1024]{1,0:T(8,128)}), f32[192,1024]{1,0:T(8,128)}) %all-reduce.27.cloned.1.call-update) | async-done | bytes 786448 | tf_op jit(solution)/shard_map/psum | solution.py:322
  284.6 36.1 %all-gather.21.cloned.1.call-done = bf16[1024,1408]{1,0:T(8,128)(2,1)} async-done(((bf16[128,1408]{1,0:T(8,128)(2,1)}), bf16[1024,1408]{1,0:T(8,128)(2,1)}) %all-gather.21.cloned.1.call-update) | async-done | bytes 2883600 | tf_op jit(solution)/shard_map/all_gather | solution.py:260
  320.7 3.6 fusion.290
  324.3 33.1 %all-gather.23.cloned.1.call-done = bf16[1024,1408]{1,0:T(8,128)(2,1)} async-done(((bf16[128,1408]{1,0:T(8,128)(2,1)}), bf16[1024,1408]{1,0:T(8,128)(2,1)}) %all-gather.23.cloned.1.call-update) | async-done | bytes 2883600 | tf_op jit(solution)/shard_map/all_gather | solution.py:261
  357.3 3.6 fusion.291
  361.0 33.0 %all-gather.25.cloned.1.call-done = bf16[1024,1408]{1,0:T(8,128)(2,1)} async-done(((bf16[128,1408]{1,0:T(8,128)(2,1)}), bf16[1024,1408]{1,0:T(8,128)(2,1)}) %all-gather.25.cloned.1.call-update) | async-done | bytes 2883600 | tf_op jit(solution)/shard_map/all_gather | solution.py:262
  394.0 4.5 multiply_convert_fusion
  405.1 31.2 %all-reduce.29.cloned.1.call-done = f32[192,1024]{1,0:T(8,128)} async-done(((f32[192,1024]{1,0:T(8,128)}), f32[192,1024]{1,0:T(8,128)}) %all-reduce.29.cloned.1.call-update) | async-done | bytes 786448 | tf_op jit(solution)/shard_map/psum | solution.py:345
  444.2 15.5 %while.103 = (s32[]{:T(128)}, f32[4,128,256]{2,1,0:T(8,128)S(1)}, f32[3,4]{1,0:T(4,128)}, f32[3,4,64,128]{3,2,1,0:T(8,128)}, f32[3,4,64,256]{3,2,1,0:T(8,128)S(1...) while((s32[]{:T(128)}, f32[4,128,256]{2,1,0:T(8,128)S(1)}, ...), condition=%wide.region_18.21_spmd.clone, body=%wide.region_17.20_spmd.clone.sunk | while | flops 353042432 | bytes 4721847 | solution.py:175
  464.2 12.6 %while.100 = (s32[]{:T(128)}, f32[4,128,256]{2,1,0:T(8,128)S(1)}, f32[3,4,128,256]{3,2,1,0:T(8,128)}, f32[3,4,64,256]{3,2,1,0:T(8,128)}, f32[3,4,1,1]{1,3,2,0:T(...) while((s32[]{:T(128)}, f32[4,128,256]{2,1,0:T(8,128)S(1)}, ...), condition=%wide.region_20.23_spmd, body=%wide.region_19.22_spmd.sunk | while | flops 201654272 | bytes 3934601 | solution.py:126
  481.0 40.6 %while.101 = (s32[]{:T(128)}, f32[4,128,256]{2,1,0:T(8,128)S(1)}, f32[3,4,64,128]{3,2,1,0:T(8,128)}, f32[3,4,64,256]{3,2,1,0:T(8,128)}, f32[3,4,64,64]{3,2,0,1:T...) while((s32[]{:T(128)}, f32[4,128,256]{2,1,0:T(8,128)S(1)}, ...), condition=%wide.region_23.26_spmd, body=%wide.region_21.25_spmd.sunk | while | flops 705495040 | bytes 15737153 | solution.py:126
  547.2 3.7 collective-permute-done.4
  568.7 3.4 convolution_bitcast_fusion.4
  573.1 4.6 fusion.294
  577.8 4.5 fusion.295
  582.4 3.8 convolution_convert_fusion
  603.0 23.6 %reduce-scatter.20.cloned.1.call-done = f32[128,512]{1,0:T(8,128)} async-done(((f32[1024,512]{1,0:T(8,128)}), f32[128,512]{1,0:T(8,128)}) %reduce-scatter.20.cloned.1.call-update) | async-done | bytes 262160 | tf_op jit(solution)/shard_map/reduce_scatter | solution.py:423
  628.2 49.2 %reduce-scatter.24.cloned.1.call-done = f32[128,1024]{1,0:T(8,128)} async-done(((f32[1024,1024]{1,0:T(8,128)}), f32[128,1024]{1,0:T(8,128)}) %reduce-scatter.24.cloned.1.call-update) | async-done | bytes 524304 | tf_op jit(solution)/shard_map/reduce_scatter | solution.py:427
  679.1 48.8 %reduce-scatter.26.cloned.1.call-done = f32[128,1024]{1,0:T(8,128)} async-done(((f32[1024,1024]{1,0:T(8,128)}), f32[128,1024]{1,0:T(8,128)}) %reduce-scatter.26.cloned.1.call-update) | async-done | bytes 524304 | tf_op jit(solution)/shard_map/reduce_scatter | solution.py:430
  729.7 48.8 %reduce-scatter.22.cloned.1.call-done = f32[128,1024]{1,0:T(8,128)} async-done(((f32[1024,1024]{1,0:T(8,128)}), f32[128,1024]{1,0:T(8,128)}) %reduce-scatter.22.cloned.1.call-update) | async-done | bytes 524304 | tf_op jit(solution)/shard_map/reduce_scatter | solution.py:424
  780.2 63.7 %reduce-scatter.32.cloned.1.call-done = f32[128,1408]{0,1:T(8,128)} async-done(((f32[1024,1408]{0,1:T(8,128)}), f32[128,1408]{0,1:T(8,128)}) %reduce-scatter.32.cloned.1.call-update) | async-done | bytes 720912 | tf_op jit(solution)/shard_map/reduce_scatter | solution.py:434
  845.8 63.5 %reduce-scatter.28.cloned.1.call-done = f32[128,1408]{1,0:T(8,128)} async-done(((f32[1024,1408]{1,0:T(8,128)}), f32[128,1408]{1,0:T(8,128)}) %reduce-scatter.28.cloned.1.call-update) | async-done | bytes 720912 | tf_op jit(solution)/shard_map/reduce_scatter | solution.py:432
  911.2 63.5 %reduce-scatter.30.cloned.1.call-done = f32[128,1408]{1,0:T(8,128)} async-done(((f32[1024,1408]{1,0:T(8,128)}), f32[128,1408]{1,0:T(8,128)}) %reduce-scatter.30.cloned.1.call-update) | async-done | bytes 720912 | tf_op jit(solution)/shard_map/reduce_scatter | solution.py:433
  978.0 4.9 psum.153
  983.1 24.2 %reduce-scatter.34.cloned.1.call-done = f32[128,4]{1,0:T(8,128)} async-done(((f32[1024,4]{1,0:T(8,128)}), f32[128,4]{1,0:T(8,128)}) %reduce-scatter.34.cloned.1.call-update) | async-done | bytes 2064
  1008.2 31.3 %reduce-scatter.36.cloned.1.call-done = f32[128,4]{1,0:T(8,128)} async-done(((f32[1024,4]{1,0:T(8,128)}), f32[128,4]{1,0:T(8,128)}) %reduce-scatter.36.cloned.1.call-update) | async-done | bytes 2064
  1040.4 32.3 %reduce-scatter.38.cloned.1.call-done = f32[256,4]{1,0:T(8,128)} async-done(((f32[2048,4]{1,0:T(8,128)}), f32[256,4]{1,0:T(8,128)}) %reduce-scatter.38.cloned.1.call-update) | async-done | bytes 4112
  1073.7 34.5 %all-reduce.31.cloned.1.call-done = (bf16[192,1024]{1,0:T(8,128)(2,1)}, bf16[192,1024]{1,0:T(8,128)(2,1)}) async-done(((bf16[192,1024]{1,0:T(8,128)(2,1)}, bf16[192,1024]{1,0:T(8,128)(2,1)}), (bf16[192,1024]{1,0:T(8,128)(2,1)}, bf16[192,1024]{1,0:T(8,128)(2,1)})) %all-reduce.31.cloned.1.call-update) | async-done | bytes 786448 | tf_op jit(solution)/shard_map/psum | solution.py:330
  1109.6 28.4 %all-reduce.18 = (bf16[1024]{0:T(1024)(128)(2,1)S(1)}, bf16[8,4]{1,0:T(8,128)(2,1)S(1)}, bf16[256]{0:T(256)(128)(2,1)S(1)}, bf16[1024]{0:T(1024)(128)(2,1)S(1)}) all-reduce(f32[1024]{0:T(1024)S(1)} %get-tuple-element.1079, f32[8,4]{1,0:T(8,128)S(1)} %broadcast_in_dim.277, ...), channel_id=2, replica_groups=mesh['fsdp'=8,'ctx'=2,'tp'=2] {'fsdp'}, use_global_device_ids=true, to_apply=%region_38.42.clone | all-reduce | flops 2336 | bytes 13504
  1138.8 5.0 all-reduce.20
  1150.6 25.9 %all-reduce.33.cloned.1.call-done = (bf16[128,1408]{0,1:T(8,128)(2,1)}, bf16[128,512]{1,0:T(8,128)(2,1)}, bf16[128,512]{1,0:T(8,128)(2,1)}, bf16[128,1024]{1,0:T...) async-done(((bf16[128,1408]{0,1:T(8,128)(2,1)}, bf16[128,512]{1,0:T(8,128)(2,1)}, ...) | async-done | bytes 2129936 | tf_op jit(solution)/shard_map/psum | solution.py:451
  (664 shorter events, 272.1 us)
Async XLA Ops:
  7.2 51.0 %copy-start = (bf16[1,192,1024]{2,1,0:T(8,128)(2,1)S(1)}, bf16[1,192,1024]{2,1,0:T(8,128)(2,1)}, u32[]{:S(2)}) copy-start(bf16[1,192,1024]{2,1,0:T(8,128)(2,1)} %param.36) | copy-start | bytes 1179652
  7.2 53.5 %copy-start.142 = (bf16[256,4]{0,1:T(4,128)(2,1)S(1)}, bf16[256,4]{0,1:T(4,128)(2,1)}, u32[]{:S(2)}) copy-start(bf16[256,4]{0,1:T(4,128)(2,1)} %param.45) | copy-start | bytes 6148
  7.2 66.3 %copy-start.144 = (bf16[128,4]{0,1:T(4,128)(2,1)S(1)}, bf16[128,4]{0,1:T(4,128)(2,1)}, u32[]{:S(2)}) copy-start(bf16[128,4]{0,1:T(4,128)(2,1)} %param.43) | copy-start | bytes 3076
  7.2 80.7 %all-gather.13.cloned.1.call-start = ((), (), s32[]{:S(2)}) async-start(), calls=%async_computation.12 | async-start | bytes 1179648 | tf_op jit(solution)/shard_map/all_gather | solution.py:251
  8.0 82.0 %all-gather.11.cloned.1.call-start = ((), (), s32[]{:S(2)}) async-start(), calls=%async_computation.11 | async-start | bytes 1179648 | tf_op jit(solution)/shard_map/all_gather | solution.py:250
  8.7 84.1 %all-gather.15.cloned.1.call-start = ((), (), s32[]{:S(2)}) async-start(), calls=%async_computation.13 | async-start | bytes 2359296 | tf_op jit(solution)/shard_map/all_gather | solution.py:252
  9.4 109.5 %all-gather.17.cloned.1.call-start = ((), (), s32[]{:S(2)}) async-start(), calls=%async_computation.14 | async-start | bytes 2359296 | tf_op jit(solution)/shard_map/all_gather | solution.py:255
  10.0 234.5 %all-gather.19.cloned.1.call-start = ((), (), s32[]{:S(2)}) async-start(), calls=%async_computation.15 | async-start | bytes 2359296 | tf_op jit(solution)/shard_map/all_gather | solution.py:258
  10.8 72.9 %collective-permute-start = (f32[3]{0:T(128)S(1)}, f32[3]{0:T(128)S(1)}, u32[]{:S(2)}, u32[]{:S(2)}) collective-permute-start(f32[3]{0:T(128)S(1)} %slice_bitcast_fusion), channel_id=1, source_target_pairs={{0,2},{1,3},{4,6},{5,7},{8,10},{9,11},{12,14},{13,15},{16,18},{17,... | collective-permute-start | bytes 44 | tf_op jit(solution)/shard_map/ppermute | solution.py:18
  15.7 267.3 %all-reduce.27.cloned.1.call-start = ((), (), s32[]{:S(2)}) async-start(), calls=%async_computation.16 | async-start | bytes 1572864 | tf_op jit(solution)/shard_map/psum | solution.py:322
  73.5 53.1 %copy-start.79 = (f32[2048,1]{0,1:T(1,128)}, f32[2048,1]{0,1:T(1,128)S(1)}, u32[]{:S(2)}) copy-start(f32[2048,1]{0,1:T(1,128)S(1)} %get-tuple-element.1240) | copy-start | bytes 24580
  73.5 53.1 %copy-start.81 = (f32[2048,1]{0,1:T(1,128)}, f32[2048,1]{0,1:T(1,128)S(1)}, u32[]{:S(2)}) copy-start(f32[2048,1]{0,1:T(1,128)S(1)} %get-tuple-element.1241) | copy-start | bytes 24580
  73.5 53.1 %copy-start.83 = (f32[2048,1]{0,1:T(1,128)}, f32[2048,1]{0,1:T(1,128)S(1)}, u32[]{:S(2)}) copy-start(f32[2048,1]{0,1:T(1,128)S(1)} %get-tuple-element.1242) | copy-start | bytes 24580
  73.5 53.1 %copy-start.85 = (f32[2048,1]{0,1:T(1,128)}, f32[2048,1]{0,1:T(1,128)S(1)}, u32[]{:S(2)}) copy-start(f32[2048,1]{0,1:T(1,128)S(1)} %get-tuple-element.1243) | copy-start | bytes 24580
  83.6 55.9 %copy-start.72 = (pred[64,64]{1,0:T(8,128)(4,1)}, pred[64,64]{1,0:T(8,128)(4,1)S(1)}, u32[]{:S(2)}) copy-start(pred[64,64]{1,0:T(8,128)(4,1)S(1)} %get-tuple-element.1271) | copy-start | bytes 12292
  83.7 55.8 %copy-start.62 = (pred[3,64,64]{2,1,0:T(8,128)(4,1)}, pred[3,64,64]{2,1,0:T(8,128)(4,1)S(1)}, u32[]{:S(2)}) copy-start(pred[3,64,64]{2,1,0:T(8,128)(4,1)S(1)} %get-tuple-element.1253) | copy-start | bytes 36868
  86.5 40.1 %copy-start.125 = (f32[192]{0:T(256)}, f32[192]{0:T(256)S(1)}, u32[]{:S(2)}) copy-start(f32[192]{0:T(256)S(1)} %get-tuple-element.1258) | copy-start | bytes 2308
  100.8 25.7 %collective-permute-start.1 = (f32[3,2048]{1,0:T(4,128)S(1)}, f32[3,2048]{1,0:T(4,128)S(1)}, u32[]{:S(2)}, u32[]{:S(2)}) collective-permute-start(f32[3,2048]{1,0:T(4,128)S(1)} %bitcast.731), channel_id=1, source_target_pairs={{0,2},{1,3},{4,6},{5,7},{8,10},{9,11},{12,14},{13,15},{16,18},{17,... | collective-permute-start | bytes 73736 | tf_op jit(solution)/shard_map/ppermute | solution.py:18
  138.7 61.8 %copy-start.26 = (f32[192,4,256]{2,0,1:T(8,128)}, f32[192,4,256]{2,0,1:T(8,128)S(1)}, u32[]{:S(2)}) copy-start(f32[192,4,256]{2,0,1:T(8,128)S(1)} %copy.342) | copy-start | bytes 2359300
  214.4 9.3 collective-permute-start.2
  248.0 72.6 %all-gather.21.cloned.1.call-start = ((), (), s32[]{:S(2)}) async-start(), calls=%async_computation.17 | async-start | bytes 3244032 | tf_op jit(solution)/shard_map/all_gather | solution.py:260
  248.8 108.5 %all-gather.23.cloned.1.call-start = ((), (), s32[]{:S(2)}) async-start(), calls=%async_computation.18 | async-start | bytes 3244032 | tf_op jit(solution)/shard_map/all_gather | solution.py:261
  249.5 144.4 %all-gather.25.cloned.1.call-start = ((), (), s32[]{:S(2)}) async-start(), calls=%async_computation.19 | async-start | bytes 3244032 | tf_op jit(solution)/shard_map/all_gather | solution.py:262
  250.3 186.0 %all-reduce.29.cloned.1.call-start = ((), (), s32[]{:S(2)}) async-start(), calls=%async_computation.20 | async-start | bytes 1572864 | tf_op jit(solution)/shard_map/psum | solution.py:345
  284.4 154.8 %copy-start.3 = (f32[192,1024]{1,0:T(8,128)}, f32[192,1024]{1,0:T(8,128)S(1)}, u32[]{:S(2)}) copy-start(f32[192,1024]{1,0:T(8,128)S(1)} %get-tuple-element.1212) | copy-start | bytes 2359300
  284.6 72.8 %copy-start.9 = (bf16[192,1024]{1,0:T(8,128)(2,1)}, bf16[192,1024]{1,0:T(8,128)(2,1)S(1)}, u32[]{:S(2)}) copy-start(bf16[192,1024]{1,0:T(8,128)(2,1)S(1)} %multiply_convert_fusion.2) | copy-start | bytes 1179652
  402.7 198.6 %reduce-scatter.18.cloned.1.call-start = ((), (), s32[]{:S(2)}) async-start(), calls=%async_computation.21 | async-start | bytes 2359296 | tf_op jit(solution)/shard_map/reduce_scatter | solution.py:422
  461.9 14.9 %collective-permute-start.3 = (bf16[4,128,256]{2,1,0:T(8,128)(2,1)}, bf16[4,128,256]{2,1,0:T(8,128)(2,1)S(1)}, u32[]{:S(2)}, u32[]{:S(2)}) collective-permute-start(bf16[4,128,256]{2,1,0:T(8,128)(2,1)} %fusion.110), channel_id=1, source_target_pairs={{2,0},{3,1},{6,4},{7,5},{10,8},{11,9},{14,12},{15,13},{18,16},{19,... | collective-permute-start | bytes 786440 | tf_op jit(solution)/shard_map/while/body/eval_jaxpr/ppermute | solution.py:18
  481.0 42.6 %copy-start.14 = (f32[4,3,1,64,64]{3,4,2,1,0:T(8,128)S(1)}, f32[4,3,1,64,64]{3,4,2,1,0:T(8,128)}, u32[]{:S(2)}) copy-start(f32[4,3,1,64,64]{3,4,2,1,0:T(8,128)} %copy-done.13) | copy-start | bytes 589828
  481.0 42.6 %copy-start.73 = (pred[64,64]{1,0:T(8,128)(4,1)S(1)}, pred[64,64]{1,0:T(8,128)(4,1)}, u32[]{:S(2)}) copy-start(pred[64,64]{1,0:T(8,128)(4,1)} %copy-done.72) | copy-start | bytes 12292
  545.1 5.8 collective-permute-start.4
  554.5 72.1 %reduce-scatter.20.cloned.1.call-start = ((), (), s32[]{:S(2)}) async-start(), calls=%async_computation.22 | async-start | bytes 2359296 | tf_op jit(solution)/shard_map/reduce_scatter | solution.py:423
  556.4 120.9 %reduce-scatter.24.cloned.1.call-start = ((), (), s32[]{:S(2)}) async-start(), calls=%async_computation.24 | async-start | bytes 4718592 | tf_op jit(solution)/shard_map/reduce_scatter | solution.py:427
  560.3 167.6 %reduce-scatter.26.cloned.1.call-start = ((), (), s32[]{:S(2)}) async-start(), calls=%async_computation.25 | async-start | bytes 4718592 | tf_op jit(solution)/shard_map/reduce_scatter | solution.py:430
  564.4 214.1 %reduce-scatter.22.cloned.1.call-start = ((), (), s32[]{:S(2)}) async-start(), calls=%async_computation.23 | async-start | bytes 4718592 | tf_op jit(solution)/shard_map/reduce_scatter | solution.py:424
  567.6 276.3 %reduce-scatter.32.cloned.1.call-start = ((), (), s32[]{:S(2)}) async-start(), calls=%async_computation.28 | async-start | bytes 6488064 | tf_op jit(solution)/shard_map/reduce_scatter | solution.py:434
  572.2 337.2 %reduce-scatter.28.cloned.1.call-start = ((), (), s32[]{:S(2)}) async-start(), calls=%async_computation.26 | async-start | bytes 6488064 | tf_op jit(solution)/shard_map/reduce_scatter | solution.py:432
  577.8 397.0 %reduce-scatter.30.cloned.1.call-start = ((), (), s32[]{:S(2)}) async-start(), calls=%async_computation.27 | async-start | bytes 6488064 | tf_op jit(solution)/shard_map/reduce_scatter | solution.py:433
  582.3 425.0 %reduce-scatter.34.cloned.1.call-start = ((), (), s32[]{:S(2)}) async-start(), calls=%async_computation.29 | async-start | bytes 589824
  592.2 447.3 %reduce-scatter.36.cloned.1.call-start = ((), (), s32[]{:S(2)}) async-start(), calls=%async_computation.30 | async-start | bytes 589824
  593.8 478.9 %reduce-scatter.38.cloned.1.call-start = ((), (), s32[]{:S(2)}) async-start(), calls=%async_computation.31 | async-start | bytes 1179648
  595.3 512.8 %all-reduce.31.cloned.1.call-start = ((), (), s32[]{:S(2)}) async-start(), calls=%async_computation.32 | async-start | bytes 1572864 | tf_op jit(solution)/shard_map/psum | solution.py:330
  601.3 575.2 %all-reduce.33.cloned.1.call-start = ((), (), s32[]{:S(2)}) async-start(), calls=%async_computation.33 | async-start | bytes 4259840 | tf_op jit(solution)/shard_map/psum | solution.py:451
  911.2 66.8 %copy-start.145 = (bf16[256]{0:T(256)(128)(2,1)S(1)}, bf16[256]{0:T(256)(128)(2,1)}, u32[]{:S(2)}) copy-start(bf16[256]{0:T(256)(128)(2,1)} %get-tuple-element.1073) | copy-start | bytes 1540
  976.6 132.9 %copy-start.115 = (f32[1024]{0:T(1024)S(1)}, f32[1024]{0:T(1024)}, u32[]{:S(2)}) copy-start(f32[1024]{0:T(1024)} %get-tuple-element.1071) | copy-start | bytes 12292
  976.6 171.0 %copy-start.134 = (f32[192]{0:T(256)S(1)}, f32[192]{0:T(256)}, u32[]{:S(2)}) copy-start(f32[192]{0:T(256)} %copy-done.133) | copy-start | bytes 2308
  976.6 171.0 %copy-start.4 = (f32[192,1024]{1,0:T(8,128)S(1)}, f32[192,1024]{1,0:T(8,128)}, u32[]{:S(2)}) copy-start(f32[192,1024]{1,0:T(8,128)} %copy-done.3) | copy-start | bytes 2359300
  1108.1 41.4 %copy-start.59 = (bf16[192,1024]{1,0:T(8,128)(2,1)S(1)}, bf16[192,1024]{1,0:T(8,128)(2,1)}, u32[]{:S(2)}) copy-start(bf16[192,1024]{1,0:T(8,128)(2,1)} %get-tuple-element.1192) | copy-start | bytes 1179652
  (132 other events, 577.7 us)
Sparse Core Ops, SparseCore 0:
  9.6 24.9 all-gather.12
  36.3 22.1 all-gather.10
  60.1 28.8 all-gather.14
  90.4 28.4 all-gather.16
  120.3 28.6 all-gather.18
  248.2 34.8 all-reduce.26
  284.7 35.9 all-gather.20
  322.3 34.9 all-gather.22
  359.0 34.9 all-gather.24
  402.9 33.3 all-reduce.28
  554.6 35.1 reduce-scatter.17
  591.9 34.5 reduce-scatter.19
  628.8 48.4 reduce-scatter.23
  679.5 48.3 reduce-scatter.25
  730.0 48.3 reduce-scatter.21
  780.6 63.2 reduce-scatter.31
  846.1 63.2 reduce-scatter.27
  911.5 63.2 reduce-scatter.29
  977.6 29.7 reduce-scatter.33
  1010.0 29.4 reduce-scatter.35
  1041.8 30.8 reduce-scatter.37
  1075.6 32.4 all-reduce.30
  1112.6 63.9 all-reduce.32
where the time goes:
time: 1200 us; the launch traced here: 1190 us
  waiting for transfers between devices  692 us (58%)
  matrix products  162 us (14%)
  other arithmetic  131 us (11%)
  blocking collectives  106 us (9%)
  local copies, waits for them, and re-layouts  68.1 us (6%)
  between operations  18.4 us (2%)
  starting transfers between devices  14.2 us (1%)
    unnamed x26, waiting for transfers between devices  92.7 us
    reduce_scatter x1, waiting for transfers between devices, per_device(): lax.psum_scatter(local_grads[13], 'fsdp', scatter_dimension=0, tiled=True)  63.7 us
    reduce_scatter x1, waiting for transfers between devices, per_device(): lax.psum_scatter(local_grads[12], 'fsdp', scatter_dimension=0, tiled=True)  63.5 us
    reduce_scatter x1, waiting for transfers between devices, per_device(): lax.psum_scatter(local_grads[11], 'fsdp', scatter_dimension=0, tiled=True)  63.5 us
    another operation x5, other arithmetic, group_prep(): lax.linalg.triangular_solve(system, (beta_blk * from_start)[..., None] *...  60.5 us
    reduce_scatter x1, waiting for transfers between devices, per_device(): lax.psum_scatter(local_grads[6], 'fsdp', scatter_dimension=0, tiled=True)  49.2 us
    reduce_scatter x1, waiting for transfers between devices, per_device(): lax.psum_scatter(local_grads[9], 'fsdp', scatter_dimension=0, tiled=True)  48.8 us
    reduce_scatter x1, waiting for transfers between devices, per_device(): lax.psum_scatter(local_grads[3], 'fsdp', scatter_dimension=0, tiled=True)  48.8 us
  transfers between devices with their start and end apart: 28, of which 20 were waited for; matrix products, arithmetic and copies ran while one was open for 20% of the time, Pallas kernels for 0%

commit v1 on v0

v1 whole, which is shorter than its diff:
```python
import jax
import jax.numpy as jnp
from jax import lax
from jax.sharding import PartitionSpec as P

DK = 128
DV = 256
LANES = 128


EPSILON = 1e-06
HIGH = lax.Precision.HIGH


def shifted(block, axis, distance):
    devices = range(lax.axis_size(axis))
    route = [(i - distance, i) for i in devices if i - distance in devices]
    return lax.ppermute(block, axis, route)


def pair_sum(block, axis):
    sent = block.astype(jnp.bfloat16)
    if lax.axis_size(axis) != 2:
        return lax.psum(sent, axis).astype(jnp.float32)
    other = lax.ppermute(sent, axis, [(0, 1), (1, 0)])
    return sent.astype(jnp.float32) + other.astype(jnp.float32)


def rms_scale(values, gain_vec):
    return (
        values * lax.rsqrt(jnp.mean(values * values, axis=-1, keepdims=True) + EPSILON) * gain_vec
    )


def unit_length(values):
    return values * lax.rsqrt(jnp.sum(values * values, axis=-1, keepdims=True) + EPSILON)


def swiglu(gate_in, up_in):
    return jax.nn.silu(gate_in) * up_in


def dot32(left, right):
    return jnp.dot(left, right, preferred_element_type=jnp.float32)


def ein(spec, left, right):
    return jnp.einsum(spec, left, right, precision=HIGH)


def unit_inverse(strict_part):
    size = strict_part.shape[-1]
    rows = lax.broadcasted_iota(jnp.int32, (size, size), 0)
    cols = lax.broadcasted_iota(jnp.int32, (size, size), 1)
    eye = (rows == cols).astype(jnp.float32)
    inverse = eye - jnp.where(rows // 2 == cols // 2, strict_part, 0.0)
    width = 2
    while width < size:
        joins = (rows // (2 * width) == cols // (2 * width)) & (rows // width != cols // width)
        middle = jnp.where(joins, strict_part, 0.0)
        inverse = inverse - ein("hij,hjk->hik", ein("hij,hjk->hik", inverse, middle), inverse)
        width *= 2
    return inverse


@jax.custom_vjp
def unit_solve(strict_part, right):
    return ein("hij,hjd->hid", unit_inverse(strict_part), right)


def unit_solve_fwd(strict_part, right):
    inverse = unit_inverse(strict_part)
    solved = ein("hij,hjd->hid", inverse, right)
    return solved, (inverse, solved)


def unit_solve_bwd(kept, d_solved):
    inverse, solved = kept
    d_right = ein("hji,hjd->hid", inverse, d_solved)
    return -ein("hid,hjd->hij", d_right, solved), d_right


unit_solve.defvjp(unit_solve_fwd, unit_solve_bwd)


def by_head(flat, head_count):
    return jnp.moveaxis(flat.reshape(flat.shape[0], head_count, -1), 1, 0)


def prepare(mixed_pre, decay_pre, beta_pre, edge_pre, taps, rate_vec, seg_value, edge_seg):
    taps_count = taps.shape[0]
    length = mixed_pre.shape[0]
    head_count = decay_pre.shape[1]
    extended = jnp.concatenate([edge_pre, mixed_pre], axis=0)
    seg_ext = jnp.concatenate([edge_seg, seg_value], axis=0)
    mixed_sum = jnp.zeros_like(mixed_pre)
    for shift_back in range(taps_count):
        offset = taps_count - 1 - shift_back
        window = extended[offset : offset + length]
        same_doc = (seg_ext[offset : offset + length] == seg_value).astype(jnp.float32)
        mixed_sum = mixed_sum + taps[shift_back] * window * same_doc[:, None]
    activated = jax.nn.silu(mixed_sum)
    width = head_count * DK
    query = unit_length(by_head(activated[:, :width], head_count)) * DK ** (-0.5)
    key = unit_length(by_head(activated[:, width : 2 * width], head_count))
    value = by_head(activated[:, 2 * width :], head_count)
    beta = jax.nn.sigmoid(beta_pre).T
    log_decay = (-rate_vec * jax.nn.softplus(decay_pre)).T
    decay_cum = jnp.cumsum(log_decay, axis=-1)
    same_doc = seg_value[:, None] == seg_value[None, :]
    rows = lax.broadcasted_iota(jnp.int32, (length, length), 0)
    cols = lax.broadcasted_iota(jnp.int32, (length, length), 1)
    lower_mask = (rows >= cols) & same_doc
    log_gap = decay_cum[:, :, None] - decay_cum[:, None, :]
    decay_pair = jnp.where(lower_mask, jnp.exp(jnp.where(lower_mask, log_gap, 0.0)), 0.0)
    decay_strict = jnp.where(rows > cols, decay_pair, 0.0)
    from_start = jnp.where(seg_value == edge_seg[-1], jnp.exp(decay_cum), 0.0)
    last_cum = decay_cum[:, -1:]
    to_end = jnp.where(seg_value == seg_value[-1], jnp.exp(last_cum - decay_cum), 0.0)
    keep_whole = jnp.where(seg_value[-1] == edge_seg[-1], jnp.exp(last_cum[:, 0]), 0.0)
    key_gram = ein("hid,hjd->hij", key, key)
    strict_part = key_gram * decay_strict * beta[:, :, None]
    right = beta[:, :, None] * jnp.concatenate([from_start[:, :, None] * key, value], axis=2)
    solved = unit_solve(strict_part, right)
    scores = ein("hid,hjd->hij", query, key) * decay_pair
    query_dec = query * from_start[:, :, None]
    key_dec = key * to_end[:, :, None]
    return solved, scores, query_dec, key_dec, keep_whole


def head_gate(outputs, gate_pre, gain_vec):
    rows = jnp.moveaxis(outputs, 0, 1)
    normed = rms_scale(rows, gain_vec)
    return (normed * jax.nn.silu(gate_pre.reshape(rows.shape))).reshape(rows.shape[0], -1)


def as_column(vector, rows):
    return jnp.pad(vector, (0, rows - vector.shape[0]))[:, None]


def gather(shard):
    return lax.all_gather(shard, "fsdp", axis=0, tiled=True)


def scatter(whole):
    return lax.psum_scatter(
        whole.astype(jnp.bfloat16), "fsdp", scatter_dimension=0, tiled=True
    )


def per_device(
    block_input,
    segments,
    norm1_gain,
    q_weight,
    k_weight,
    v_weight,
    decay_weight,
    beta_weight,
    gate_weight,
    conv_weight,
    decay_rate,
    head_gain,
    out_weight,
    norm2_gain,
    ffn_gate,
    ffn_up,
    ffn_down,
    cotangent,
):
    fsdp = lax.axis_size("fsdp")
    ctx = lax.axis_size("ctx")
    rows = q_weight.shape[0]
    head_count = decay_weight.shape[1]
    taps_count = conv_weight.shape[1]
    q_cols = q_weight.shape[1]
    qk_cols = q_cols + k_weight.shape[1]
    pre_cols = qk_cols + v_weight.shape[1]
    gate_cols = gate_weight.shape[1]
    ffn_cols = ffn_gate.shape[1]
    small = [
        decay_weight,
        beta_weight,
        norm1_gain[:, None],
        norm2_gain[:, None],
        as_column(head_gain, rows),
        conv_weight.reshape(rows, -1),
    ]
    small_used = sum(piece.shape[1] for piece in small)
    small_cols = -(-small_used // LANES) * LANES
    small.append(jnp.zeros((rows, small_cols - small_used), jnp.bfloat16))
    first_shard = jnp.concatenate([q_weight, k_weight, v_weight] + small, axis=1)
    first_mat = gather(first_shard)
    second_shard, _ = lax.optimization_barrier((jnp.concatenate([gate_weight, out_weight], axis=1), first_shard))
    second_mat = gather(second_shard)
    third_mat = gather(jnp.concatenate([ffn_gate, ffn_up], axis=1))
    down_mat = gather(ffn_down)
    gate_mat, out_mat = second_mat[:, :gate_cols], second_mat[:, gate_cols:]
    small_mat = first_mat[:, pre_cols:]
    heads2 = 2 * head_count
    gain_one = small_mat[:, heads2].astype(jnp.float32)
    gain_two = small_mat[:, heads2 + 1].astype(jnp.float32)
    head_len = head_gain.shape[0]
    gain_head = (
        small_mat[:, heads2 + 2].reshape(fsdp, rows)[:, :head_len].reshape(-1).astype(jnp.float32)
    )
    conv_cols = conv_weight.shape[0] * taps_count // rows
    conv_taps = small_mat[:, heads2 + 3 : heads2 + 3 + conv_cols].reshape(-1, taps_count)

    row_input = block_input[0]
    seg_value = segments[0].astype(jnp.float32)
    row_cot = cotangent[0]
    length = row_input.shape[0]
    tail_start = length - taps_count + 1
    input_wide = row_input.astype(jnp.float32)
    norm_one, norm_one_back = jax.vjp(rms_scale, input_wide, gain_one)
    normed_one = norm_one.astype(jnp.bfloat16)
    projected = dot32(normed_one, first_mat)
    mixed_pre = projected[:, :pre_cols]
    decay_pre = projected[:, pre_cols : pre_cols + head_count]
    beta_pre = projected[:, pre_cols + head_count : pre_cols + heads2]
    edge_pre, edge_seg = shifted((mixed_pre[tail_start:], seg_value[tail_start:]), "ctx", 1)

    def to_taps(by_channel):
        grouped = by_channel.T.reshape(taps_count, head_count, -1)
        return jnp.concatenate(
            [
                grouped[:, :, :DK].reshape(taps_count, -1),
                grouped[:, :, DK : 2 * DK].reshape(taps_count, -1),
                grouped[:, :, 2 * DK :].reshape(taps_count, -1),
            ],
            axis=1,
        )

    def prepare_local(mixed_in, decay_in, beta_in, edge_in, taps_in, rate_in):
        return prepare(
            mixed_in, decay_in, beta_in, edge_in, to_taps(taps_in), rate_in, seg_value, edge_seg
        )

    (solved, scores, query_dec, key_dec, keep_whole), prepare_back = jax.vjp(
        prepare_local,
        mixed_pre,
        decay_pre,
        beta_pre,
        edge_pre,
        conv_taps.astype(jnp.float32),
        decay_rate,
    )
    wide_keys, new_values = solved[:, :, :DK], solved[:, :, DK:]
    state_zero = jnp.zeros((head_count, DK, DV), jnp.float32)
    carried = ein("hcd,hce->hde", key_dec, new_values)
    if ctx > 2:
        moved = keep_whole[:, None, None] * jnp.eye(DK, dtype=jnp.float32) - ein(
            "hcd,hce->hde", key_dec, wide_keys
        )

    def pass_on(total, distance):
        return shifted(total.astype(jnp.bfloat16), "ctx", distance).astype(jnp.float32)

    state_start = pass_on(carried, 1) if ctx > 1 else state_zero
    for _ in range(ctx - 2):
        state_start = pass_on(ein("hde,hef->hdf", moved, state_start) + carried, 1)
    gate_pre = dot32(normed_one, gate_mat)
    fresh = new_values - ein("hcd,hde->hce", wide_keys, state_start)
    outputs = ein("hcd,hde->hce", query_dec, state_start) + ein("hcj,hje->hce", scores, fresh)
    gated, gate_back = jax.vjp(head_gate, outputs, gate_pre, gain_head)
    gated_half = gated.astype(jnp.bfloat16)
    mixer_out = pair_sum(dot32(gated_half, out_mat.T), "tp")
    hidden = input_wide + mixer_out
    norm_two, norm_two_back = jax.vjp(rms_scale, hidden, gain_two)
    normed_two = norm_two.astype(jnp.bfloat16)
    both_ffn = dot32(normed_two, third_mat)
    product, swiglu_back = jax.vjp(swiglu, both_ffn[:, :ffn_cols], both_ffn[:, ffn_cols:])
    hidden_units = product.astype(jnp.bfloat16)
    d_units = dot32(row_cot, down_mat)
    d_gate_ffn, d_up_ffn = swiglu_back(d_units)
    d_both_half = jnp.concatenate(
        [d_gate_ffn.astype(jnp.bfloat16), d_up_ffn.astype(jnp.bfloat16)], axis=1
    )
    d_normed_two = pair_sum(dot32(d_both_half, third_mat.T), "tp")
    ffn_out = pair_sum(dot32(hidden_units, down_mat.T), "tp")
    block_out = (hidden + ffn_out).astype(jnp.bfloat16)
    g_down = dot32(row_cot.T, hidden_units)
    g_both = dot32(normed_two.T, d_both_half)
    ffn_shards = scatter(jnp.concatenate([g_down.astype(jnp.bfloat16), g_both.astype(jnp.bfloat16)], axis=1))
    d_hidden_two, g_gain_two = norm_two_back(d_normed_two)
    d_hidden = row_cot.astype(jnp.float32) + d_hidden_two
    d_hidden_half = d_hidden.astype(jnp.bfloat16)
    d_gated = dot32(d_hidden_half, out_mat)
    d_outputs, d_gate_pre, g_head_part = gate_back(d_gated)
    d_gate_half = d_gate_pre.astype(jnp.bfloat16)
    g_out = dot32(d_hidden_half.T, gated_half)
    g_gate = dot32(normed_one.T, d_gate_half)
    second_shards = scatter(jnp.concatenate([g_gate.astype(jnp.bfloat16), g_out.astype(jnp.bfloat16)], axis=1))

    d_fresh_local = ein("hcj,hce->hje", scores, d_outputs)
    local_start = ein("hcd,hce->hde", query_dec, d_outputs) - ein(
        "hcd,hce->hde", wide_keys, d_fresh_local
    )
    state_grad = pass_on(local_start, -1) if ctx > 1 else state_zero
    for _ in range(ctx - 2):
        state_grad = pass_on(ein("hed,hef->hdf", moved, state_grad) + local_start, -1)
    d_fresh = d_fresh_local + ein("hcd,hde->hce", key_dec, state_grad)
    d_solved = jnp.concatenate([-ein("hce,hde->hcd", d_fresh, state_start), d_fresh], axis=2)
    d_scores = ein("hce,hje->hcj", d_outputs, fresh)
    d_query_dec = ein("hce,hde->hcd", d_outputs, state_start)
    d_key_dec = ein("hce,hde->hcd", fresh, state_grad)
    d_keep = jnp.sum(state_start * state_grad, axis=(1, 2))
    d_mixed, d_decay, d_beta, d_edge, g_conv, g_rate = prepare_back(
        (d_solved, d_scores, d_query_dec, d_key_dec, d_keep)
    )
    edge_grad = shifted(d_edge, "ctx", -1)
    d_mixed = d_mixed + jnp.pad(edge_grad, ((tail_start, 0), (0, 0)))
    half_first = jnp.concatenate(
        [
            d_mixed.astype(jnp.bfloat16),
            d_decay.astype(jnp.bfloat16),
            d_beta.astype(jnp.bfloat16),
            jnp.zeros((length, small_cols - heads2), jnp.bfloat16),
        ],
        axis=1,
    )
    d_first_part = dot32(half_first, first_mat.T) + dot32(d_gate_half, gate_mat.T)
    d_normed_one = pair_sum(d_first_part, "tp")
    g_first = dot32(normed_one.T, half_first[:, : pre_cols + heads2])
    d_input_one, _ = norm_one_back(d_normed_one)
    _, g_gain_one = norm_one_back(d_first_part)
    input_grad = d_hidden + d_input_one
    head_part = jnp.pad(g_head_part.reshape(fsdp, head_len), ((0, 0), (0, rows - head_len)))
    extra = jnp.concatenate(
        [
            g_gain_one[:, None],
            g_gain_two[:, None],
            head_part.reshape(-1, 1),
            g_conv.reshape(fsdp * rows, -1),
            jnp.broadcast_to(g_rate[None], (fsdp * rows, head_count)),
        ],
        axis=1,
    )
    pad_cols = small_cols - heads2 - extra.shape[1]
    first_shards = scatter(
        jnp.concatenate(
            [
                g_first.astype(jnp.bfloat16),
                jnp.pad(extra, ((0, 0), (0, pad_cols))).astype(jnp.bfloat16),
            ],
            axis=1,
        )
    )
    ffn_sum = pair_sum(ffn_shards, "ctx")
    second_sum = pair_sum(second_shards, "ctx")
    first_sum = pair_sum(first_shards, "ctx")
    small_sum = first_sum[:, pre_cols:]
    shared = pair_sum(small_sum[:, heads2 : heads2 + 3], "tp")
    conv_end = heads2 + 3 + conv_cols
    return (
        block_out[None],
        input_grad[None],
        shared[:, 0],
        first_sum[:, :q_cols],
        first_sum[:, q_cols:qk_cols],
        first_sum[:, qk_cols:pre_cols],
        small_sum[:, :head_count],
        small_sum[:, head_count:heads2],
        second_sum[:, :gate_cols],
        small_sum[:, heads2 + 3 : conv_end].reshape(conv_weight.shape),
        small_sum[0, conv_end : conv_end + head_count],
        shared[:head_len, 2],
        second_sum[:, gate_cols:],
        small_sum[:, heads2 + 1],
        ffn_sum[:, ffn_cols : 2 * ffn_cols],
        ffn_sum[:, 2 * ffn_cols :],
        ffn_sum[:, :ffn_cols],
    )


def solution(mesh):
    placed = (
        P("fsdp", "ctx", None),
        P("fsdp", "ctx"),
        P("fsdp"),
        P("fsdp", "tp"),
        P("fsdp", "tp"),
        P("fsdp", "tp"),
        P("fsdp", "tp"),
        P("fsdp", "tp"),
        P("fsdp", "tp"),
        P(("tp", "fsdp"), None),
        P("tp"),
        P("fsdp"),
        P("fsdp", "tp"),
        P("fsdp"),
        P("fsdp", "tp"),
        P("fsdp", "tp"),
        P("fsdp", "tp"),
        P("fsdp", "ctx", None),
    )
    return jax.shard_map(
        per_device,
        mesh=mesh,
        in_specs=placed,
        out_specs=(
            P("fsdp", "ctx", None),
            P("fsdp", "ctx", None),
            P("fsdp"),
            P("fsdp", "tp"),
            P("fsdp", "tp"),
            P("fsdp", "tp"),
            P("fsdp", "tp"),
            P("fsdp", "tp"),
            P("fsdp", "tp"),
            P(("tp", "fsdp"), None),
            P("tp"),
            P("fsdp"),
            P("fsdp", "tp"),
            P("fsdp"),
            P("fsdp", "tp"),
            P("fsdp", "tp"),
            P("fsdp", "tp"),
        ),
        check_vma=False,
    )
```

time: 1200 us -> 531 us (0.44)
  waiting for transfers between devices: 692 us -> 263 us
  blocking collectives: 106 us -> 0 us
  matrix products: 162 us -> 85.8 us
  other arithmetic: 131 us -> 63.5 us
  starting transfers between devices: 14.2 us -> 26.2 us
    reduce_scatter x8 -> x1, waiting for transfers between devices: 361 us -> 77 us  [scatter(): lax.psum_scatter(whole.astype(jnp.bfloat16), 'fsdp', scatter_dimension=0,...]
    psum x4 -> x0, waiting for transfers between devices: 114 us -> none  [the longest x1 34.5 us: per_device(): lax.psum(jnp.dot(hidden_units, down_ffn_mat.T, preferred_element_type=jnp...]
    dot_general x102 -> x50, matrix products: 153 us -> 85.8 us  [the longest x15 46.8 us: dot32(): return jnp.dot(left, right, preferred_element_type=jnp.float32)]
    unnamed x26 -> x9, waiting for transfers between devices: 92.7 us -> 27 us
    another operation x8 -> x7, other arithmetic: 63.2 us -> 6.43 us  [the longest x5 60.5 us: group_prep(): lax.linalg.triangular_solve(system, (beta_blk * from_start)[..., None] *...]
    all_gather x5 -> x0, blocking collectives: 51.3 us -> none  [the longest x1 12.8 us: per_device(): lax.all_gather(shards[7], 'fsdp', axis=0, tiled=True)]
    ppermute x0 -> x8, waiting for transfers between devices: none -> 49.5 us  [pair_sum(): other = lax.ppermute(sent, axis, [(0, 1), (1, 0)])]
    unnamed x2 -> x0, blocking collectives: 45 us -> none
  transfers between devices with their start and end apart: 28 -> 20, of which waited for: 20 -> 12; matrix products, arithmetic and copies ran while one was open for 20% -> 32% of each run, Pallas kernels for 0% -> 0%
where the time goes in v1:
time: 531 us; the launch traced here: 524 us
  waiting for transfers between devices  263 us (50%)
  matrix products  85.8 us (16%)
  local copies, waits for them, and re-layouts  67.2 us (13%)
  other arithmetic  63.5 us (12%)
  starting transfers between devices  26.2 us (5%)
  between operations  18 us (3%)
    all_gather x4, waiting for transfers between devices, gather(): return lax.all_gather(shard, 'fsdp', axis=0, tiled=True)  105 us
    reduce_scatter x1, waiting for transfers between devices, scatter(): lax.psum_scatter(whole.astype(jnp.bfloat16), 'fsdp', scatter_dimension=0,...  77 us
    ppermute x8, waiting for transfers between devices, pair_sum(): other = lax.ppermute(sent, axis, [(0, 1), (1, 0)])  49.5 us
    dot_general x15, matrix products, dot32(): return jnp.dot(left, right, preferred_element_type=jnp.float32)  46.8 us
    unnamed x311, local copies, waits for them, and re-layouts  36.9 us
    dot_general x33, matrix products, ein(): return jnp.einsum(spec, left, right, precision=HIGH)  34.5 us
    unnamed x9, waiting for transfers between devices  27 us
    ppermute x8, starting transfers between devices, pair_sum(): other = lax.ppermute(sent, axis, [(0, 1), (1, 0)])  13.2 us
  transfers between devices with their start and end apart: 20, of which 12 were waited for; matrix products, arithmetic and copies ran while one was open for 32% of the time, Pallas kernels for 0%

profile of v1, /device:TPU:0, one launch (start us, length us, event | category | flops | bytes accessed | tf_op | source)
XLA Modules:
  0.0 524.1 jit_solution(13226841630451052815)
XLA Ops:
  12.2 1.9 pad_maximum_fusion.9
  17.9 4.9 collective-permute-start.1
  28.1 1.9 broadcast_compare_fusion
  30.0 35.7 %all-gather.7.cloned.1.call-done = bf16[1024,2048]{1,0:T(8,128)(2,1)} async-done(((bf16[128,2048]{1,0:T(8,128)(2,1)}), bf16[1024,2048]{1,0:T(8,128)(2,1)}) %all-gather.7.cloned.1.call-update) | async-done | bytes 4194320 | tf_op jit(solution)/shard_map/all_gather | solution.py:142
  65.8 3.1 slice_bitcast_fusion
  68.8 3.9 copy.451
  72.8 43.1 %all-gather.5.cloned.1.call-done = bf16[1024,2176]{1,0:T(8,128)(2,1)} async-done(((bf16[128,2176]{1,0:T(8,128)(2,1)}), bf16[1024,2176]{1,0:T(8,128)(2,1)}) %all-gather.5.cloned.1.call-update) | async-done | bytes 4456464 | tf_op jit(solution)/shard_map/all_gather | solution.py:142
  118.6 3.4 fusion.195
  123.2 3.4 collective-permute-start
  131.3 3.5 fusion.104
  135.9 2.5 fusion.14
  159.7 5.1 collective-permute-done.2
  171.6 8.9 %collective-permute-done.3 = bf16[192,1024]{1,0:T(8,128)(2,1)S(1)} collective-permute-done((bf16[192,1024]{1,0:T(8,128)(2,1)S(1)}, bf16[192,1024]{1,0:T(8,128)(2,1)S(1)}, u32[]{:S(2)}, u32[]{:S(2)}) %collective-permute-start.3) | collective-permute-done | bytes 393248 | tf_op jit(solution)/shard_map/ppermute | solution.py:25
  181.9 5.4 %fusion.241 = f32[192,2816]{1,0:T(8,128)} fusion(bf16[1024,2816]{1,0:T(8,128)(2,1)} %all-gather.9.cloned.1.call-done, f32[192,1024]{1,0:T(8,128)S(1)} %get-tuple-element.142, f32[1024]{0:T(1024)S(1)} %get-tuple-element.121, f32[192]{0:T(256)} %fusion.210), kind=kOutput, calls=%fused_computation.429 | convolution fusion | flops 1107886080 | bytes 8721152 | tf_op jit(solution)/shard_map/dot_general | solution.py:44
  187.4 26.0 %all-gather.11.cloned.1.call-done = bf16[1024,1408]{1,0:T(8,128)(2,1)} async-done(((bf16[128,1408]{1,0:T(8,128)(2,1)}), bf16[1024,1408]{1,0:T(8,128)(2,1)}) %all-gather.11.cloned.1.call-update) | async-done | bytes 2883600 | tf_op jit(solution)/shard_map/all_gather | solution.py:142
  213.4 4.5 fusion.28
  217.9 2.8 convolution_convert_fusion.5
  223.5 3.1 convolution_convert_fusion.6
  227.2 5.8 %collective-permute-done.5 = bf16[192,1024]{1,0:T(8,128)(2,1)} collective-permute-done((bf16[192,1024]{1,0:T(8,128)(2,1)}, bf16[192,1024]{1,0:T(8,128)(2,1)}, u32[]{:S(2)}, u32[]{:S(2)}) %collective-permute-start.5) | collective-permute-done | bytes 393248 | tf_op jit(solution)/shard_map/ppermute | solution.py:25
  234.5 6.0 %collective-permute-done.4 = bf16[192,1024]{1,0:T(8,128)(2,1)S(1)} collective-permute-done((bf16[192,1024]{1,0:T(8,128)(2,1)S(1)}, bf16[192,1024]{1,0:T(8,128)(2,1)S(1)}, u32[]{:S(2)}, u32[]{:S(2)}) %collective-permute-start.4) | collective-permute-done | bytes 393248 | tf_op jit(solution)/shard_map/ppermute | solution.py:25
  240.6 2.3 fusion.43
  251.6 2.1 convolution_convert_fusion.3
  254.5 1.9 multiply_reduce_fusion.14
  257.0 2.4 fusion.19
  264.0 1.9 convolution_convert_fusion.4
  265.9 2.4 pad_maximum_fusion.1
  268.2 6.5 %copy.521 = bf16[1024,2048]{1,0:T(8,128)(2,1)} copy(bf16[1024,2048]{0,1:T(8,128)(2,1)} %pad_maximum_fusion.1) | data formatting | bytes 8388608
  274.9 3.5 fusion.7
  285.8 2.8 multiply_reduce_fusion.7
  289.5 2.2 multiply_reduce_fusion.15
  292.1 1.8 multiply_reduce_fusion.3
  302.3 5.0 reduce-window.16
  309.5 4.3 pad_add_fusion
  316.1 5.0 fusion.259
  323.6 3.4 convolution_convert_fusion.1
  327.0 4.6 collective-permute-done.8
  333.2 3.8 fusion.1
  337.0 6.5 %copy.519 = bf16[1024,2176]{1,0:T(8,128)(2,1)} copy(bf16[1024,2176]{0,1:T(8,128)(2,1)} %fusion.1) | data formatting | bytes 8912896
  344.7 2.5 fusion.2
  347.2 4.7 copy.475
  351.9 4.3 convolution_convert_fusion
  356.3 7.6 %pad_maximum_fusion = bf16[1024,4224]{1,0:T(8,128)(2,1)} fusion(bf16[1024,2816]{1,0:T(8,128)(2,1)} %convolution_convert_fusion, bf16[1024,1408]{1,0:T(8,128)(2,1)} %copy.475), kind=kLoop, calls=%fused_computation.2 | loop fusion | flops 17301504 | bytes 17301504 | tf_op jit(solution)/shard_map/concatenate | solution.py:285
  365.3 3.6 collective-permute-start.11
  369.0 2.2 fusion.49
  371.1 26.2 %reduce-scatter.10.cloned.1.call-done = bf16[128,2176]{1,0:T(8,128)(2,1)} async-done(((bf16[1024,2176]{1,0:T(8,128)(2,1)}), bf16[128,2176]{1,0:T(8,128)(2,1)}) %reduce-scatter.10.cloned.1.call-update) | async-done | bytes 557072
  402.4 8.9 %collective-permute-done.9 = bf16[128,2176]{0,1:T(8,128)(2,1)} collective-permute-done((bf16[128,2176]{0,1:T(8,128)(2,1)S(1)}, bf16[128,2176]{0,1:T(8,128)(2,1)}, u32[]{:S(2)}, u32[]{:S(2)}) %collective-permute-start.9) | collective-permute-done | bytes 557088 | tf_op jit(solution)/shard_map/ppermute | solution.py:25
  413.1 77.0 %reduce-scatter.8.cloned.1.call-done = bf16[128,4224]{1,0:T(8,128)(2,1)} async-done(((bf16[1024,4224]{1,0:T(8,128)(2,1)}), bf16[128,4224]{1,0:T(8,128)(2,1)}) %reduce-scatter.8.cloned.1.call-update) | async-done | bytes 1081360 | tf_op jit(solution)/shard_map/reduce_scatter | solution.py:146
  498.9 15.3 %collective-permute-done.12 = bf16[128,4224]{1,0:T(8,128)(2,1)} collective-permute-done((bf16[128,4224]{1,0:T(8,128)(2,1)}, bf16[128,4224]{1,0:T(8,128)(2,1)}, u32[]{:S(2)}, u32[]{:S(2)}) %collective-permute-start.12) | collective-permute-done | bytes 1081376 | tf_op jit(solution)/shard_map/ppermute | solution.py:25
  (517 shorter events, 116.6 us)
Async XLA Ops:
  7.2 58.6 %all-gather.7.cloned.1.call-start = ((), (), s32[]{:S(2)}) async-start(), calls=%async_computation.4 | async-start | bytes 4718592 | tf_op jit(solution)/shard_map/all_gather | solution.py:142
  16.0 8.3 %copy-start = (bf16[1,192,1024]{2,1,0:T(8,128)(2,1)S(1)}, bf16[1,192,1024]{2,1,0:T(8,128)(2,1)}, u32[]{:S(2)}) copy-start(bf16[1,192,1024]{2,1,0:T(8,128)(2,1)} %param.18) | copy-start | bytes 1179652
  16.0 99.8 %all-gather.5.cloned.1.call-start = ((), (), s32[]{:S(2)}) async-start(), calls=%async_computation.3 | async-start | bytes 5013504 | tf_op jit(solution)/shard_map/all_gather | solution.py:142
  16.8 165.2 %all-gather.9.cloned.1.call-start = ((), (), s32[]{:S(2)}) async-start(), calls=%async_computation.5 | async-start | bytes 6488064 | tf_op jit(solution)/shard_map/all_gather | solution.py:142
  17.8 195.6 %all-gather.11.cloned.1.call-start = ((), (), s32[]{:S(2)}) async-start(), calls=%async_computation.6 | async-start | bytes 3244032 | tf_op jit(solution)/shard_map/all_gather | solution.py:142
  17.9 9.5 %collective-permute-start.1 = (f32[3]{0:T(128)S(1)}, f32[3]{0:T(128)S(1)}, u32[]{:S(2)}, u32[]{:S(2)}) collective-permute-start(f32[3]{0:T(128)S(1)} %slice_bitcast_fusion.6), channel_id=1, source_target_pairs={{0,2},{1,3},{4,6},{5,7},{8,10},{9,11},{12,14},{13,15},{16,18},{17,... | collective-permute-start | bytes 44 | tf_op jit(solution)/shard_map/ppermute | solution.py:18
  22.8 341.1 %reduce-scatter.12.cloned.1.call-start = ((), (), s32[]{:S(2)}) async-start(), calls=%async_computation.9 | async-start | bytes 4718592
  24.4 44.4 %copy-start.132 = (f32[192]{0:T(256)}, f32[192]{0:T(256)S(1)}, u32[]{:S(2)}) copy-start(f32[192]{0:T(256)S(1)} %fusion.39) | copy-start | bytes 2308
  24.5 106.8 %copy-start.80 = (f32[192]{0:T(256)}, f32[192]{0:T(256)S(1)}, u32[]{:S(2)}) copy-start(f32[192]{0:T(256)S(1)} %fusion.209) | copy-start | bytes 2308
  24.5 102.6 %copy-start.141 = (f32[4]{0:T(128)}, f32[4]{0:T(128)S(1)}, u32[]{:S(2)}) copy-start(f32[4]{0:T(128)S(1)} %neg.42) | copy-start | bytes 52
  30.0 105.8 %copy-start.122 = (f32[192]{0:T(256)}, f32[192]{0:T(256)S(1)}, u32[]{:S(2)}) copy-start(f32[192]{0:T(256)S(1)} %get-tuple-element.202) | copy-start | bytes 2308
  30.0 105.8 %copy-start.124 = (f32[192]{0:T(256)}, f32[192]{0:T(256)S(1)}, u32[]{:S(2)}) copy-start(f32[192]{0:T(256)S(1)} %get-tuple-element.203) | copy-start | bytes 2308
  123.2 12.5 %collective-permute-start = (f32[3,2048]{1,0:T(4,128)S(1)}, f32[3,2048]{1,0:T(4,128)S(1)}, u32[]{:S(2)}, u32[]{:S(2)}) collective-permute-start(f32[3,2048]{1,0:T(4,128)S(1)} %slice.260), channel_id=1, source_target_pairs={{0,2},{1,3},{4,6},{5,7},{8,10},{9,11},{12,14},{13,15},{16,18},{17,... | collective-permute-start | bytes 73736 | tf_op jit(solution)/shard_map/ppermute | solution.py:18
  127.1 8.7 %copy-start.72 = (f32[1,2048]{1,0:T(1,128)}, f32[1,2048]{1,0:T(1,128)S(1)}, u32[]{:S(2)}) copy-start(f32[1,2048]{1,0:T(1,128)S(1)} %get-tuple-element.181) | copy-start | bytes 24580
  127.1 8.7 %copy-start.74 = (f32[1,2048]{1,0:T(1,128)}, f32[1,2048]{1,0:T(1,128)S(1)}, u32[]{:S(2)}) copy-start(f32[1,2048]{1,0:T(1,128)S(1)} %get-tuple-element.182) | copy-start | bytes 24580
  127.1 8.7 %copy-start.76 = (f32[1,2048]{1,0:T(1,128)}, f32[1,2048]{1,0:T(1,128)S(1)}, u32[]{:S(2)}) copy-start(f32[1,2048]{1,0:T(1,128)S(1)} %get-tuple-element.183) | copy-start | bytes 24580
  127.2 8.7 %copy-start.78 = (f32[1,2048]{1,0:T(1,128)}, f32[1,2048]{1,0:T(1,128)S(1)}, u32[]{:S(2)}) copy-start(f32[1,2048]{1,0:T(1,128)S(1)} %get-tuple-element.184) | copy-start | bytes 24580
  129.9 8.8 %copy-start.70 = (f32[1,4,2,128]{3,1,2,0:T(4,128)}, f32[1,4,2,128]{3,1,2,0:T(4,128)S(1)}, u32[]{:S(2)}) copy-start(f32[1,4,2,128]{3,1,2,0:T(4,128)S(1)} %copy.599) | copy-start | bytes 12292
  130.0 12.3 %copy-start.85 = (f32[4,192]{1,0:T(4,128)}, f32[4,192]{1,0:T(4,128)S(1)}, u32[]{:S(2)}) copy-start(f32[4,192]{1,0:T(4,128)S(1)} %fusion.232) | copy-start | bytes 9220
  139.1 12.7 %copy-start.82 = (f32[4,192]{1,0:T(4,128)}, f32[4,192]{1,0:T(4,128)S(1)}, u32[]{:S(2)}) copy-start(f32[4,192]{1,0:T(4,128)S(1)} %get-tuple-element.144) | copy-start | bytes 9220
  139.1 17.5 %copy-start.100 = (f32[4,192]{1,0:T(4,128)}, f32[4,192]{1,0:T(4,128)S(1)}, u32[]{:S(2)}) copy-start(f32[4,192]{1,0:T(4,128)S(1)} %get-tuple-element.187) | copy-start | bytes 9220
  139.1 27.2 %copy-start.102 = (f32[4,192]{1,0:T(4,128)}, f32[4,192]{1,0:T(4,128)S(1)}, u32[]{:S(2)}) copy-start(f32[4,192]{1,0:T(4,128)S(1)} %get-tuple-element.143) | copy-start | bytes 9220
  139.7 13.1 %copy-start.38 = (f32[4,192,192]{1,2,0:T(8,128)}, f32[4,192,192]{1,2,0:T(8,128)S(1)}, u32[]{:S(2)}) copy-start(f32[4,192,192]{1,2,0:T(8,128)S(1)} %fusion.238) | copy-start | bytes 1769476
  156.6 8.2 %copy-start.8 = (f32[4,192,384]{2,1,0:T(8,128)}, f32[4,192,384]{2,1,0:T(8,128)S(1)}, u32[]{:S(2)}) copy-start(f32[4,192,384]{2,1,0:T(8,128)S(1)} %fusion.24) | copy-start | bytes 3538948
  157.5 7.3 %collective-permute-start.2 = (bf16[4,128,256]{2,1,0:T(8,128)(2,1)S(1)}, bf16[4,128,256]{2,1,0:T(8,128)(2,1)S(1)}, u32[]{:S(2)}, u32[]{:S(2)}) collective-permute-start(bf16[4,128,256]{2,1,0:T(8,128)(2,1)S(1)} %convolution_convert_fusion.7), channel_id=1, source_target_pairs={{0,2},{1,3},{4,6},{5,7},{8,10},{9,11},{12,14},{13,15},{16,18},{17,... | collective-permute-start | bytes 786440 | tf_op jit(solution)/shard_map/ppermute | solution.py:18
  170.0 10.5 %collective-permute-start.3 = (bf16[192,1024]{1,0:T(8,128)(2,1)S(1)}, bf16[192,1024]{1,0:T(8,128)(2,1)S(1)}, u32[]{:S(2)}, u32[]{:S(2)}) collective-permute-start(bf16[192,1024]{1,0:T(8,128)(2,1)S(1)} %fusion.16), channel_id=1, source_target_pairs={{0,1},{1,0},{2,3},{3,2},{4,5},{5,4},{6,7},{7,6},{8,9},{9,8},{10,11... | collective-permute-start | bytes 1179656 | tf_op jit(solution)/shard_map/ppermute | solution.py:25
  220.7 12.3 %collective-permute-start.5 = (bf16[192,1024]{1,0:T(8,128)(2,1)}, bf16[192,1024]{1,0:T(8,128)(2,1)}, u32[]{:S(2)}, u32[]{:S(2)}) collective-permute-start(bf16[192,1024]{1,0:T(8,128)(2,1)} %convolution_convert_fusion.5), channel_id=1, source_target_pairs={{0,1},{1,0},{2,3},{3,2},{4,5},{5,4},{6,7},{7,6},{8,9},{9,8},{10,11... | collective-permute-start | bytes 1179656 | tf_op jit(solution)/shard_map/ppermute | solution.py:25
  223.4 9.5 %copy-start.90 = (f32[192]{0:T(256)S(1)}, f32[192]{0:T(256)}, u32[]{:S(2)}) copy-start(f32[192]{0:T(256)} %fusion.210) | copy-start | bytes 2308
  226.6 14.0 %copy-start.44 = (bf16[1,192,1024]{2,1,0:T(8,128)(2,1)S(1)}, bf16[1,192,1024]{2,1,0:T(8,128)(2,1)}, u32[]{:S(2)}) copy-start(bf16[1,192,1024]{2,1,0:T(8,128)(2,1)} %param.35) | copy-start | bytes 1179652
  226.6 14.0 %collective-permute-start.4 = (bf16[192,1024]{1,0:T(8,128)(2,1)S(1)}, bf16[192,1024]{1,0:T(8,128)(2,1)S(1)}, u32[]{:S(2)}, u32[]{:S(2)}) collective-permute-start(bf16[192,1024]{1,0:T(8,128)(2,1)S(1)} %convolution_convert_fusion.6), channel_id=1, source_target_pairs={{0,1},{1,0},{2,3},{3,2},{4,5},{5,4},{6,7},{7,6},{8,9},{9,8},{10,11... | collective-permute-start | bytes 1179656 | tf_op jit(solution)/shard_map/ppermute | solution.py:25
  233.0 9.8 %copy-start.35 = (bf16[1024,2048]{1,0:T(8,128)(2,1)S(1)}, bf16[1024,2048]{1,0:T(8,128)(2,1)}, u32[]{:S(2)}) copy-start(bf16[1024,2048]{1,0:T(8,128)(2,1)} %all-gather.7.cloned.1.call-done) | copy-start | bytes 12582916
  242.8 8.8 %copy-start.13 = (f32[192,1024]{1,0:T(8,128)}, f32[192,1024]{1,0:T(8,128)S(1)}, u32[]{:S(2)}) copy-start(f32[192,1024]{1,0:T(8,128)S(1)} %get-tuple-element.177) | copy-start | bytes 2359300
  248.9 8.1 %copy-start.23 = (f32[4,192,256]{2,1,0:T(8,128)}, f32[4,192,256]{2,1,0:T(8,128)S(1)}, u32[]{:S(2)}) copy-start(f32[4,192,256]{2,1,0:T(8,128)S(1)} %fusion.74) | copy-start | bytes 2359300
  259.4 19.5 %collective-permute-start.6 = (bf16[4,128,256]{2,1,0:T(8,128)(2,1)}, bf16[4,128,256]{2,1,0:T(8,128)(2,1)}, u32[]{:S(2)}, u32[]{:S(2)}) collective-permute-start(bf16[4,128,256]{2,1,0:T(8,128)(2,1)} %fusion.19), channel_id=1, source_target_pairs={{2,0},{3,1},{6,4},{7,5},{10,8},{11,9},{14,12},{15,13},{18,16},{19,... | collective-permute-start | bytes 786440 | tf_op jit(solution)/shard_map/ppermute | solution.py:18
  274.8 122.5 %reduce-scatter.10.cloned.1.call-start = ((), (), s32[]{:S(2)}) async-start(), calls=%async_computation.8 | async-start | bytes 5013504
  296.8 11.0 %copy-start.142 = (f32[4]{0:T(128)S(1)}, f32[4]{0:T(128)}, u32[]{:S(2)}) copy-start(f32[4]{0:T(128)} %copy-done.141) | copy-start | bytes 52
  296.8 12.6 %copy-start.111 = (f32[192,4]{0,1:T(4,128)S(1)}, f32[192,4]{0,1:T(4,128)}, u32[]{:S(2)}) copy-start(f32[192,4]{0,1:T(4,128)} %copy-done.110) | copy-start | bytes 9220
  296.8 12.6 %copy-start.114 = (f32[4,192]{1,0:T(4,128)S(1)}, f32[4,192]{1,0:T(4,128)}, u32[]{:S(2)}) copy-start(f32[4,192]{1,0:T(4,128)} %get-tuple-element.157) | copy-start | bytes 9220
  296.8 12.6 %copy-start.121 = (f32[4,192]{1,0:T(4,128)S(1)}, f32[4,192]{1,0:T(4,128)}, u32[]{:S(2)}) copy-start(f32[4,192]{1,0:T(4,128)} %get-tuple-element.167) | copy-start | bytes 9220
  296.8 17.2 %collective-permute-start.7 = (f32[3,2048]{1,0:T(4,128)S(1)}, f32[3,2048]{1,0:T(4,128)}, u32[]{:S(2)}, u32[]{:S(2)}) collective-permute-start(f32[3,2048]{1,0:T(4,128)S(1)} %pad_add_fusion.1), channel_id=1, source_target_pairs={{2,0},{3,1},{6,4},{7,5},{10,8},{11,9},{14,12},{15,13},{18,16},{19,... | collective-permute-start | bytes 73736 | tf_op jit(solution)/shard_map/ppermute | solution.py:18
  321.1 10.5 %collective-permute-start.8 = (bf16[192,1024]{1,0:T(8,128)(2,1)S(1)}, bf16[192,1024]{1,0:T(8,128)(2,1)}, u32[]{:S(2)}, u32[]{:S(2)}) collective-permute-start(bf16[192,1024]{1,0:T(8,128)(2,1)S(1)} %get-tuple-element.212), channel_id=1, source_target_pairs={{0,1},{1,0},{2,3},{3,2},{4,5},{5,4},{6,7},{7,6},{8,9},{9,8},{10,11... | collective-permute-start | bytes 1179656 | tf_op jit(solution)/shard_map/ppermute | solution.py:25
  323.6 8.0 %copy-start.42 = (f32[192,1024]{1,0:T(8,128)S(1)}, f32[192,1024]{1,0:T(8,128)}, u32[]{:S(2)}) copy-start(f32[192,1024]{1,0:T(8,128)} %get-tuple-element.213) | copy-start | bytes 2359300
  343.5 146.6 %reduce-scatter.8.cloned.1.call-start = ((), (), s32[]{:S(2)}) async-start(), calls=%async_computation.7 | async-start | bytes 9732096 | tf_op jit(solution)/shard_map/reduce_scatter | solution.py:146
  365.3 34.9 %collective-permute-start.11 = (bf16[128,2048]{0,1:T(8,128)(2,1)S(1)}, bf16[128,2048]{0,1:T(8,128)(2,1)S(1)}, u32[]{:S(2)}, u32[]{:S(2)}) collective-permute-start(bf16[128,2048]{0,1:T(8,128)(2,1)S(1)} %copy.522), channel_id=1, source_target_pairs={{0,2},{2,0},{1,3},{3,1},{4,6},{6,4},{5,7},{7,5},{8,10},{10,8},{9,1... | collective-permute-start | bytes 1572872 | tf_op jit(solution)/shard_map/ppermute | solution.py:25
  398.7 12.7 %collective-permute-start.9 = (bf16[128,2176]{0,1:T(8,128)(2,1)S(1)}, bf16[128,2176]{0,1:T(8,128)(2,1)}, u32[]{:S(2)}, u32[]{:S(2)}) collective-permute-start(bf16[128,2176]{0,1:T(8,128)(2,1)S(1)} %copy.520), channel_id=1, source_target_pairs={{0,2},{2,0},{1,3},{3,1},{4,6},{6,4},{5,7},{7,5},{8,10},{10,8},{9,1... | collective-permute-start | bytes 1671176 | tf_op jit(solution)/shard_map/ppermute | solution.py:25
  490.1 24.0 %collective-permute-start.12 = (bf16[128,4224]{1,0:T(8,128)(2,1)}, bf16[128,4224]{1,0:T(8,128)(2,1)}, u32[]{:S(2)}, u32[]{:S(2)}) collective-permute-start(bf16[128,4224]{1,0:T(8,128)(2,1)} %reduce-scatter.8.cloned.1.call-done), channel_id=1, source_target_pairs={{0,2},{2,0},{1,3},{3,1},{4,6},{6,4},{5,7},{7,5},{8,10},{10,8},{9,1... | collective-permute-start | bytes 3244040 | tf_op jit(solution)/shard_map/ppermute | solution.py:25
  492.1 5.7 %collective-permute-start.10 = (bf16[128,3]{0,1:T(4,128)(2,1)S(1)}, bf16[128,3]{0,1:T(4,128)(2,1)S(1)}, u32[]{:S(2)}, u32[]{:S(2)}) collective-permute-start(bf16[128,3]{0,1:T(4,128)(2,1)S(1)} %slice.389), channel_id=1, source_target_pairs={{0,1},{1,0},{2,3},{3,2},{4,5},{5,4},{6,7},{7,6},{8,9},{9,8},{10,11... | collective-permute-start | bytes 2312 | tf_op jit(solution)/shard_map/ppermute | solution.py:25
  494.3 19.9 %copy-start.51 = (bf16[128,4224]{1,0:T(8,128)(2,1)S(1)}, bf16[128,4224]{1,0:T(8,128)(2,1)}, u32[]{:S(2)}) copy-start(bf16[128,4224]{1,0:T(8,128)(2,1)} %reduce-scatter.8.cloned.1.call-done) | copy-start | bytes 3244036
  (118 other events, 328.2 us)
Sparse Core Ops, SparseCore 0:
  16.1 49.5 all-gather.6
  68.0 47.8 all-gather.4
  118.0 59.1 all-gather.8
  178.7 34.6 all-gather.10
  274.9 50.8 reduce-scatter.11
  343.7 53.6 reduce-scatter.9
  399.6 90.4 reduce-scatter.7

commit v2 on v1

--- a/solution.py
+++ b/solution.py
@@ -3,6 +3,7 @@
 from jax import lax
 from jax.sharding import PartitionSpec as P
 
+
 DK = 128
 DV = 256
 LANES = 128
@@ -19,7 +20,7 @@
 
 
 def pair_sum(block, axis):
-    sent = block.astype(jnp.bfloat16)
+    sent = lax.optimization_barrier(block.astype(jnp.bfloat16))
     if lax.axis_size(axis) != 2:
         return lax.psum(sent, axis).astype(jnp.float32)
     other = lax.ppermute(sent, axis, [(0, 1), (1, 0)])
@@ -106,7 +107,7 @@
     value = by_head(activated[:, 2 * width :], head_count)
     beta = jax.nn.sigmoid(beta_pre).T
     log_decay = (-rate_vec * jax.nn.softplus(decay_pre)).T
-    decay_cum = jnp.cumsum(log_decay, axis=-1)
+    decay_cum = running_sum(log_decay)
     same_doc = seg_value[:, None] == seg_value[None, :]
     rows = lax.broadcasted_iota(jnp.int32, (length, length), 0)
     cols = lax.broadcasted_iota(jnp.int32, (length, length), 1)
@@ -146,6 +147,18 @@
     return lax.psum_scatter(
         whole.astype(jnp.bfloat16), "fsdp", scatter_dimension=0, tiled=True
     )
+
+
+def dot16(left, right):
+    return jnp.dot(left, right, preferred_element_type=jnp.bfloat16)
+
+
+def running_sum(values):
+    size = values.shape[-1]
+    rows = lax.broadcasted_iota(jnp.int32, (size, size), 0)
+    cols = lax.broadcasted_iota(jnp.int32, (size, size), 1)
+    upper = (rows <= cols).astype(jnp.float32)
+    return jnp.dot(values, upper, precision=lax.Precision.HIGHEST)
 
 
 def per_device(
@@ -176,7 +189,6 @@
     q_cols = q_weight.shape[1]
     qk_cols = q_cols + k_weight.shape[1]
     pre_cols = qk_cols + v_weight.shape[1]
-    gate_cols = gate_weight.shape[1]
     ffn_cols = ffn_gate.shape[1]
     small = [
         decay_weight,
@@ -191,11 +203,10 @@
     small.append(jnp.zeros((rows, small_cols - small_used), jnp.bfloat16))
     first_shard = jnp.concatenate([q_weight, k_weight, v_weight] + small, axis=1)
     first_mat = gather(first_shard)
-    second_shard, _ = lax.optimization_barrier((jnp.concatenate([gate_weight, out_weight], axis=1), first_shard))
-    second_mat = gather(second_shard)
+    gate_mat = gather(gate_weight)
+    out_mat = gather(out_weight)
     third_mat = gather(jnp.concatenate([ffn_gate, ffn_up], axis=1))
     down_mat = gather(ffn_down)
-    gate_mat, out_mat = second_mat[:, :gate_cols], second_mat[:, gate_cols:]
     small_mat = first_mat[:, pre_cols:]
     heads2 = 2 * head_count
     gain_one = small_mat[:, heads2].astype(jnp.float32)
@@ -277,21 +288,27 @@
     d_both_half = jnp.concatenate(
         [d_gate_ffn.astype(jnp.bfloat16), d_up_ffn.astype(jnp.bfloat16)], axis=1
     )
-    d_normed_two = pair_sum(dot32(d_both_half, third_mat.T), "tp")
+    units_wide = jnp.pad(hidden_units, ((0, 0), (0, -ffn_cols % (2 * LANES))))
+    g_down = dot16(row_cot.T, units_wide)
+    down_shards = scatter(g_down)
+    d_normed_part = dot32(d_both_half, third_mat.T).astype(jnp.bfloat16)
+    g_both = dot16(normed_two.T, d_both_half)
+    both_shards = scatter(g_both)
+    d_normed_two = pair_sum(d_normed_part, "tp")
+    d_normed_two, _, _ = lax.optimization_barrier((d_normed_two, g_both, g_down))
     ffn_out = pair_sum(dot32(hidden_units, down_mat.T), "tp")
     block_out = (hidden + ffn_out).astype(jnp.bfloat16)
-    g_down = dot32(row_cot.T, hidden_units)
-    g_both = dot32(normed_two.T, d_both_half)
-    ffn_shards = scatter(jnp.concatenate([g_down.astype(jnp.bfloat16), g_both.astype(jnp.bfloat16)], axis=1))
     d_hidden_two, g_gain_two = norm_two_back(d_normed_two)
     d_hidden = row_cot.astype(jnp.float32) + d_hidden_two
     d_hidden_half = d_hidden.astype(jnp.bfloat16)
     d_gated = dot32(d_hidden_half, out_mat)
     d_outputs, d_gate_pre, g_head_part = gate_back(d_gated)
     d_gate_half = d_gate_pre.astype(jnp.bfloat16)
-    g_out = dot32(d_hidden_half.T, gated_half)
-    g_gate = dot32(normed_one.T, d_gate_half)
-    second_shards = scatter(jnp.concatenate([g_gate.astype(jnp.bfloat16), g_out.astype(jnp.bfloat16)], axis=1))
+    g_out = dot16(d_hidden_half.T, gated_half)
+    out_shards = scatter(g_out)
+    g_gate = dot16(normed_one.T, d_gate_half)
+    gate_shards = scatter(g_gate)
+    d_outputs, _, _ = lax.optimization_barrier((d_outputs, g_out, g_gate))
 
     d_fresh_local = ein("hcj,hce->hje", scores, d_outputs)
     local_start = ein("hcd,hce->hde", query_dec, d_outputs) - ein(
@@ -310,6 +327,7 @@
         (d_solved, d_scores, d_query_dec, d_key_dec, d_keep)
     )
     edge_grad = shifted(d_edge, "ctx", -1)
+    rate_sum = lax.psum(g_rate, ("fsdp", "ctx"))
     d_mixed = d_mixed + jnp.pad(edge_grad, ((tail_start, 0), (0, 0)))
     half_first = jnp.concatenate(
         [
@@ -322,7 +340,6 @@
     )
     d_first_part = dot32(half_first, first_mat.T) + dot32(d_gate_half, gate_mat.T)
     d_normed_one = pair_sum(d_first_part, "tp")
-    g_first = dot32(normed_one.T, half_first[:, : pre_cols + heads2])
     d_input_one, _ = norm_one_back(d_normed_one)
     _, g_gain_one = norm_one_back(d_first_part)
     input_grad = d_hidden + d_input_one
@@ -333,22 +350,19 @@
             g_gain_two[:, None],
             head_part.reshape(-1, 1),
             g_conv.reshape(fsdp * rows, -1),
-            jnp.broadcast_to(g_rate[None], (fsdp * rows, head_count)),
         ],
         axis=1,
     )
-    pad_cols = small_cols - heads2 - extra.shape[1]
-    first_shards = scatter(
-        jnp.concatenate(
-            [
-                g_first.astype(jnp.bfloat16),
-                jnp.pad(extra, ((0, 0), (0, pad_cols))).astype(jnp.bfloat16),
-            ],
-            axis=1,
-        )
-    )
-    ffn_sum = pair_sum(ffn_shards, "ctx")
-    second_sum = pair_sum(second_shards, "ctx")
+    wide_half = jnp.pad(half_first, ((0, 0), (0, -half_first.shape[1] % (2 * LANES))))
+    g_first = dot16(normed_one.T, wide_half)
+    g_first = lax.dynamic_update_slice(
+        g_first, extra.astype(jnp.bfloat16), (0, pre_cols + heads2)
+    )
+    first_shards = scatter(g_first)
+    down_sum = pair_sum(down_shards, "ctx")
+    both_sum = pair_sum(both_shards, "ctx")
+    out_sum = pair_sum(out_shards, "ctx")
+    gate_sum = pair_sum(gate_shards, "ctx")
     first_sum = pair_sum(first_shards, "ctx")
     small_sum = first_sum[:, pre_cols:]
     shared = pair_sum(small_sum[:, heads2 : heads2 + 3], "tp")
@@ -362,15 +376,15 @@
         first_sum[:, qk_cols:pre_cols],
         small_sum[:, :head_count],
         small_sum[:, head_count:heads2],
-        second_sum[:, :gate_cols],
+        gate_sum,
         small_sum[:, heads2 + 3 : conv_end].reshape(conv_weight.shape),
-        small_sum[0, conv_end : conv_end + head_count],
+        rate_sum,
         shared[:head_len, 2],
-        second_sum[:, gate_cols:],
+        out_sum,
         small_sum[:, heads2 + 1],
-        ffn_sum[:, ffn_cols : 2 * ffn_cols],
-        ffn_sum[:, 2 * ffn_cols :],
-        ffn_sum[:, :ffn_cols],
+        both_sum[:, :ffn_cols],
+        both_sum[:, ffn_cols:],
+        down_sum[:, :ffn_cols],
     )
 
 

time: 531 us -> 520 us (0.979)
  blocking collectives: 0 us -> 31.6 us
  other arithmetic: 63.5 us -> 38.1 us
  local copies, waits for them, and re-layouts: 67.2 us -> 45.8 us
  waiting for transfers between devices: 263 us -> 270 us
    psum x0 -> x1, blocking collectives: none -> 31.6 us  [per_device(): rate_sum = lax.psum(g_rate, ('fsdp', 'ctx'))]
    unnamed x9 -> x11, waiting for transfers between devices: 27 us -> 2.01 us
    reduce_scatter x1 -> x4, waiting for transfers between devices: 77 us -> 97.4 us  [scatter(): lax.psum_scatter(whole.astype(jnp.bfloat16), 'fsdp', scatter_dimension=0,...]
    unnamed x311 -> x262, local copies, waits for them, and re-layouts: 36.9 us -> 17.9 us
    dot_general x15 -> x10, matrix products: 46.8 us -> 29.1 us  [dot32(): return jnp.dot(left, right, preferred_element_type=jnp.float32)]
    dot_general x0 -> x7, matrix products: none -> 16.9 us  [the longest x5 16.4 us: dot16(): return jnp.dot(left, right, preferred_element_type=jnp.bfloat16)]
    concatenate x4 -> x1, other arithmetic: 15.8 us -> 0.35 us  [per_device(): jnp.concatenate([g_gain_one[:, None], g_gain_two[:, None], head_part.resh...]
    all_gather x4 -> x5, waiting for transfers between devices: 105 us -> 117 us  [gather(): return lax.all_gather(shard, 'fsdp', axis=0, tiled=True)]
  transfers between devices with their start and end apart: 20 -> 25, of which waited for: 12 -> 16; matrix products, arithmetic and copies ran while one was open for 32% -> 29% of each run, Pallas kernels for 0% -> 0%
where the time goes in v2:
time: 520 us; the launch traced here: 515 us
  waiting for transfers between devices  270 us (52%)
  matrix products  85.5 us (16%)
  local copies, waits for them, and re-layouts  45.8 us (9%)
  other arithmetic  38.1 us (7%)
  blocking collectives  31.6 us (6%)
  starting transfers between devices  26.5 us (5%)
  between operations  17.7 us (3%)
    all_gather x5, waiting for transfers between devices, gather(): return lax.all_gather(shard, 'fsdp', axis=0, tiled=True)  117 us
    reduce_scatter x4, waiting for transfers between devices, scatter(): lax.psum_scatter(whole.astype(jnp.bfloat16), 'fsdp', scatter_dimension=0,...  97.4 us
    ppermute x10, waiting for transfers between devices, pair_sum(): other = lax.ppermute(sent, axis, [(0, 1), (1, 0)])  42 us
    dot_general x33, matrix products, ein(): return jnp.einsum(spec, left, right, precision=HIGH)  36.3 us
    psum x1, blocking collectives, per_device(): rate_sum = lax.psum(g_rate, ('fsdp', 'ctx'))  31.6 us
    dot_general x10, matrix products, dot32(): return jnp.dot(left, right, preferred_element_type=jnp.float32)  29.1 us
    unnamed x262, local copies, waits for them, and re-layouts  17.9 us
    dot_general x5, matrix products, dot16(): return jnp.dot(left, right, preferred_element_type=jnp.bfloat16)  16.4 us
  transfers between devices with their start and end apart: 25, of which 16 were waited for; matrix products, arithmetic and copies ran while one was open for 29% of the time, Pallas kernels for 0%

profile of v2, /device:TPU:0, one launch (start us, length us, event | category | flops | bytes accessed | tf_op | source)
XLA Modules:
  0.0 515.4 jit_solution(3717754512621465418)
XLA Ops:
  12.9 1.9 concatenate.31
  16.8 4.9 collective-permute-start.1
  26.9 1.9 broadcast_compare_fusion
  28.8 12.8 %all-gather.8.cloned.1.call-done = bf16[1024,1024]{1,0:T(8,128)(2,1)} async-done(((bf16[128,1024]{1,0:T(8,128)(2,1)}), bf16[1024,1024]{1,0:T(8,128)(2,1)}) %all-gather.8.cloned.1.call-update) | async-done | bytes 2097168 | tf_op jit(solution)/shard_map/all_gather | solution.py:143
  41.6 4.0 copy.327
  45.5 46.7 %all-gather.6.cloned.1.call-done = bf16[1024,2176]{1,0:T(8,128)(2,1)} async-done(((bf16[128,2176]{1,0:T(8,128)(2,1)}), bf16[1024,2176]{1,0:T(8,128)(2,1)}) %all-gather.6.cloned.1.call-update) | async-done | bytes 4456464 | tf_op jit(solution)/shard_map/all_gather | solution.py:143
  95.1 3.4 fusion.191
  101.0 3.5 collective-permute-start
  104.8 2.4 fusion.95
  109.3 5.9 %fusion.5 = (f32[192,2048]{1,0:T(8,128)S(1)}, f32[192,2048]{1,0:T(8,128)}) fusion(f32[192]{0:T(256)S(1)} %copy-done.96, f32[192,2048]{1,0:T(8,128)} %slice.210, f32[3,2048]{1,0:T(4,128)S(1)} %collective-permute-done, f32[2048]{0:T(1024)S(1)} %bitcast.364, f32[192]{0:T(256)S(1)} %get-tuple-element.183, f32[2048]{0:T(1024)S(1)} %bitcast.366, ...), kind=kLoop, calls=%fused_computation.20 | loop fusion | flops 7077888 | bytes 4779008 | tf_op jit(solution)/shard_map/jvp(jit(silu))/mul | solution.py:103
  116.6 1.7 fusion.53
  136.3 5.1 collective-permute-done.2
  143.9 2.6 convolution_convert_fusion.2
  148.1 9.0 %collective-permute-done.3 = bf16[192,1024]{1,0:T(8,128)(2,1)S(1)} collective-permute-done((bf16[192,1024]{1,0:T(8,128)(2,1)S(1)}, bf16[192,1024]{1,0:T(8,128)(2,1)S(1)}, u32[]{:S(2)}, u32[]{:S(2)}) %collective-permute-start.3) | collective-permute-done | bytes 393248 | tf_op jit(solution)/shard_map/ppermute | solution.py:26
  157.3 26.3 %all-gather.12.cloned.1.call-done = bf16[1024,2816]{1,0:T(8,128)(2,1)} async-done(((bf16[128,2816]{1,0:T(8,128)(2,1)}), bf16[1024,2816]{1,0:T(8,128)(2,1)}) %all-gather.12.cloned.1.call-update) | async-done | bytes 5767184 | tf_op jit(solution)/shard_map/all_gather | solution.py:143
  183.6 5.4 %fusion.257 = f32[192,2816]{1,0:T(8,128)} fusion(bf16[1024,2816]{1,0:T(8,128)(2,1)} %all-gather.12.cloned.1.call-done, f32[192,1024]{1,0:T(8,128)S(1)} %get-tuple-element.127, f32[1024]{0:T(1024)S(1)} %get-tuple-element.106, f32[192]{0:T(256)S(1)} %fusion.223), kind=kOutput, calls=%fused_computation.435 | convolution fusion | flops 1107886080 | bytes 8721152 | tf_op jit(solution)/shard_map/dot_general | solution.py:45
  189.0 30.8 %all-gather.14.cloned.1.call-done = bf16[1024,1408]{1,0:T(8,128)(2,1)} async-done(((bf16[128,1408]{1,0:T(8,128)(2,1)}), bf16[1024,1408]{1,0:T(8,128)(2,1)}) %all-gather.14.cloned.1.call-update) | async-done | bytes 2883600 | tf_op jit(solution)/shard_map/all_gather | solution.py:143
  219.8 3.6 fusion.16
  223.9 2.8 convolution_convert_fusion
  228.2 1.8 convolution_convert_fusion.1
  230.0 2.7 convolution_bitcast_fusion
  233.3 4.3 fusion.62
  241.1 5.6 %collective-permute-done.4 = bf16[192,1024]{1,0:T(8,128)(2,1)} collective-permute-done((bf16[192,1024]{1,0:T(8,128)(2,1)}, bf16[192,1024]{1,0:T(8,128)(2,1)}, u32[]{:S(2)}, u32[]{:S(2)}) %collective-permute-start.4) | collective-permute-done | bytes 393248 | tf_op jit(solution)/shard_map/ppermute | solution.py:26
  246.7 2.2 fusion.33
  250.6 1.7 fusion.34
  253.1 2.1 fusion.97
  255.3 3.5 fusion.163
  260.1 3.0 copy.390
  267.1 1.9 fusion.69
  274.0 2.4 multiply_reduce_fusion.14
  276.4 1.7 fusion.7
  279.8 1.7 fusion.278
  282.7 5.1 collective-permute-done.6
  294.1 2.1 multiply_reduce_fusion.7
  297.1 2.9 multiply_reduce_fusion.15
  302.1 5.1 multiply_reduce_fusion.3
  308.0 1.7 collective-permute-start.7
  311.7 2.2 collective-permute-done.7
  316.3 4.8 fusion.275
  323.2 3.7 fusion.25
  326.9 3.1 collective-permute-done.8
  330.9 3.9 dynamic_update_slice.3
  335.5 31.6 %psum.7 = f32[4]{0:T(128)} all-reduce(f32[4]{0:T(128)S(1)} %neg.47), channel_id=1, replica_groups=mesh['fsdp'=8,'ctx'=2,'tp'=2] {'fsdp','ctx'}, use_global_device_ids=true, to_apply=%region_29.30 | all-reduce | flops 4 | bytes 32 | tf_op jit(solution)/shard_map/psum | solution.py:330
  373.1 3.5 collective-permute-done.11
  377.4 47.9 %reduce-scatter.8.cloned.1.call-done = bf16[128,2304]{1,0:T(8,128)(2,1)} async-done(((bf16[1024,2304]{1,0:T(8,128)(2,1)}), bf16[128,2304]{1,0:T(8,128)(2,1)}) %reduce-scatter.8.cloned.1.call-update) | async-done | bytes 589840 | tf_op jit(solution)/shard_map/reduce_scatter | solution.py:147
  428.9 9.9 %collective-permute-done.9 = bf16[128,2304]{1,0:T(8,128)(2,1)S(1)} collective-permute-done((bf16[128,2304]{1,0:T(8,128)(2,1)}, bf16[128,2304]{1,0:T(8,128)(2,1)S(1)}, u32[]{:S(2)}, u32[]{:S(2)}) %collective-permute-start.9) | collective-permute-done | bytes 589856 | tf_op jit(solution)/shard_map/ppermute | solution.py:26
  441.3 49.5 %reduce-scatter.14.cloned.1.call-done = bf16[128,2816]{1,0:T(8,128)(2,1)} async-done(((bf16[1024,2816]{1,0:T(8,128)(2,1)}), bf16[128,2816]{1,0:T(8,128)(2,1)}) %reduce-scatter.14.cloned.1.call-update) | async-done | bytes 720912 | tf_op jit(solution)/shard_map/reduce_scatter | solution.py:147
  497.3 9.6 %collective-permute-done.13 = bf16[128,2816]{1,0:T(8,128)(2,1)S(1)} collective-permute-done((bf16[128,2816]{1,0:T(8,128)(2,1)}, bf16[128,2816]{1,0:T(8,128)(2,1)S(1)}, u32[]{:S(2)}, u32[]{:S(2)}) %collective-permute-start.13) | collective-permute-done | bytes 720928 | tf_op jit(solution)/shard_map/ppermute | solution.py:26
  (457 shorter events, 102.1 us)
Async XLA Ops:
  7.2 8.5 %copy-start.54 = (bf16[128,1408]{1,0:T(8,128)(2,1)S(1)}, bf16[128,1408]{1,0:T(8,128)(2,1)}, u32[]{:S(2)}) copy-start(bf16[128,1408]{1,0:T(8,128)(2,1)} %param.33) | copy-start | bytes 1081348
  7.2 8.5 %copy-start.55 = (bf16[128,1408]{1,0:T(8,128)(2,1)S(1)}, bf16[128,1408]{1,0:T(8,128)(2,1)}, u32[]{:S(2)}) copy-start(bf16[128,1408]{1,0:T(8,128)(2,1)} %param.32) | copy-start | bytes 1081348
  7.2 34.4 %all-gather.8.cloned.1.call-start = ((), (), s32[]{:S(2)}) async-start(), calls=%async_computation.6 | async-start | bytes 2359296 | tf_op jit(solution)/shard_map/all_gather | solution.py:143
  7.9 84.3 %all-gather.6.cloned.1.call-start = ((), (), s32[]{:S(2)}) async-start(), calls=%async_computation.5 | async-start | bytes 5013504 | tf_op jit(solution)/shard_map/all_gather | solution.py:143
  14.9 8.9 %copy-start = (bf16[1,192,1024]{2,1,0:T(8,128)(2,1)S(1)}, bf16[1,192,1024]{2,1,0:T(8,128)(2,1)}, u32[]{:S(2)}) copy-start(bf16[1,192,1024]{2,1,0:T(8,128)(2,1)} %param.18) | copy-start | bytes 1179652
  14.9 129.0 %all-gather.10.cloned.1.call-start = ((), (), s32[]{:S(2)}) async-start(), calls=%async_computation.7 | async-start | bytes 2359296 | tf_op jit(solution)/shard_map/all_gather | solution.py:143
  15.6 168.0 %all-gather.12.cloned.1.call-start = ((), (), s32[]{:S(2)}) async-start(), calls=%async_computation.8 | async-start | bytes 6488064 | tf_op jit(solution)/shard_map/all_gather | solution.py:143
  16.6 203.2 %all-gather.14.cloned.1.call-start = ((), (), s32[]{:S(2)}) async-start(), calls=%async_computation.9 | async-start | bytes 3244032 | tf_op jit(solution)/shard_map/all_gather | solution.py:143
  16.8 9.5 %collective-permute-start.1 = (f32[3]{0:T(128)S(1)}, f32[3]{0:T(128)S(1)}, u32[]{:S(2)}, u32[]{:S(2)}) collective-permute-start(f32[3]{0:T(128)S(1)} %slice_bitcast_fusion.3), channel_id=1, source_target_pairs={{0,2},{1,3},{4,6},{5,7},{8,10},{9,11},{12,14},{13,15},{16,18},{17,... | collective-permute-start | bytes 44 | tf_op jit(solution)/shard_map/ppermute | solution.py:19
  21.7 345.4 %reduce-scatter.10.cloned.1.call-start = ((), (), s32[]{:S(2)}) async-start(), calls=%async_computation.11 | async-start | bytes 2359296 | tf_op jit(solution)/shard_map/reduce_scatter | solution.py:147
  23.2 106.6 %copy-start.58 = (pred[192,192]{0,1:T(8,128)(4,1)}, pred[192,192]{0,1:T(8,128)(4,1)S(1)}, u32[]{:S(2)}) copy-start(pred[192,192]{0,1:T(8,128)(4,1)S(1)} %get-tuple-element.203) | copy-start | bytes 110596
  23.9 21.6 %copy-start.102 = (f32[192]{0:T(256)}, f32[192]{0:T(256)S(1)}, u32[]{:S(2)}) copy-start(f32[192]{0:T(256)S(1)} %fusion.29) | copy-start | bytes 2308
  23.9 228.4 %copy-start.71 = (f32[192]{0:T(256)}, f32[192]{0:T(256)S(1)}, u32[]{:S(2)}) copy-start(f32[192]{0:T(256)S(1)} %fusion.222) | copy-start | bytes 2308
  24.0 117.7 %copy-start.50 = (pred[192,192]{0,1:T(8,128)(4,1)}, pred[192,192]{0,1:T(8,128)(4,1)S(1)}, u32[]{:S(2)}) copy-start(pred[192,192]{0,1:T(8,128)(4,1)S(1)} %fusion.187) | copy-start | bytes 110596
  28.8 80.4 %copy-start.94 = (f32[192]{0:T(256)}, f32[192]{0:T(256)S(1)}, u32[]{:S(2)}) copy-start(f32[192]{0:T(256)S(1)} %get-tuple-element.183) | copy-start | bytes 2308
  98.5 9.2 %copy-start.8 = (f32[192,2176]{1,0:T(8,128)}, f32[192,2176]{1,0:T(8,128)S(1)}, u32[]{:S(2)}) copy-start(f32[192,2176]{1,0:T(8,128)S(1)} %fusion.191) | copy-start | bytes 5013508
  101.0 8.2 %collective-permute-start = (f32[3,2048]{1,0:T(4,128)}, f32[3,2048]{1,0:T(4,128)S(1)}, u32[]{:S(2)}, u32[]{:S(2)}) collective-permute-start(f32[3,2048]{1,0:T(4,128)} %slice.212), channel_id=1, source_target_pairs={{0,2},{1,3},{4,6},{5,7},{8,10},{9,11},{12,14},{13,15},{16,18},{17,... | collective-permute-start | bytes 73736 | tf_op jit(solution)/shard_map/ppermute | solution.py:19
  104.8 27.2 %copy-start.75 = (f32[4,192]{1,0:T(4,128)}, f32[4,192]{1,0:T(4,128)S(1)}, u32[]{:S(2)}) copy-start(f32[4,192]{1,0:T(4,128)S(1)} %fusion.248) | copy-start | bytes 9220
  115.3 20.3 %copy-start.2 = (f32[24,4,8,128]{3,2,1,0:T(8,128)}, f32[24,4,8,128]{3,2,1,0:T(8,128)S(1)}, u32[]{:S(2)}) copy-start(f32[24,4,8,128]{3,2,1,0:T(8,128)S(1)} %get-tuple-element.146) | copy-start | bytes 1179652
  115.3 27.6 %copy-start.5 = (f32[24,4,8,128]{3,2,1,0:T(8,128)}, f32[24,4,8,128]{3,2,1,0:T(8,128)S(1)}, u32[]{:S(2)}) copy-start(f32[24,4,8,128]{3,2,1,0:T(8,128)S(1)} %get-tuple-element.145) | copy-start | bytes 1179652
  115.9 12.9 %copy-start.73 = (f32[4,192]{1,0:T(4,128)}, f32[4,192]{1,0:T(4,128)S(1)}, u32[]{:S(2)}) copy-start(f32[4,192]{1,0:T(4,128)S(1)} %get-tuple-element.129) | copy-start | bytes 9220
  115.9 17.2 %copy-start.84 = (f32[4,192]{1,0:T(4,128)}, f32[4,192]{1,0:T(4,128)S(1)}, u32[]{:S(2)}) copy-start(f32[4,192]{1,0:T(4,128)S(1)} %get-tuple-element.169) | copy-start | bytes 9220
  115.9 26.9 %copy-start.86 = (f32[4,192]{1,0:T(4,128)}, f32[4,192]{1,0:T(4,128)S(1)}, u32[]{:S(2)}) copy-start(f32[4,192]{1,0:T(4,128)S(1)} %get-tuple-element.128) | copy-start | bytes 9220
  116.6 13.2 %copy-start.35 = (f32[4,192,192]{1,2,0:T(8,128)}, f32[4,192,192]{1,2,0:T(8,128)S(1)}, u32[]{:S(2)}) copy-start(f32[4,192,192]{1,2,0:T(8,128)S(1)} %fusion.254) | copy-start | bytes 1769476
  134.1 7.2 %collective-permute-start.2 = (bf16[4,128,256]{2,1,0:T(8,128)(2,1)S(1)}, bf16[4,128,256]{2,1,0:T(8,128)(2,1)S(1)}, u32[]{:S(2)}, u32[]{:S(2)}) collective-permute-start(bf16[4,128,256]{2,1,0:T(8,128)(2,1)S(1)} %convolution_convert_fusion.3), channel_id=1, source_target_pairs={{0,2},{1,3},{4,6},{5,7},{8,10},{9,11},{12,14},{13,15},{16,18},{17,... | collective-permute-start | bytes 786440 | tf_op jit(solution)/shard_map/ppermute | solution.py:19
  146.5 10.5 %collective-permute-start.3 = (bf16[192,1024]{1,0:T(8,128)(2,1)S(1)}, bf16[192,1024]{1,0:T(8,128)(2,1)S(1)}, u32[]{:S(2)}, u32[]{:S(2)}) collective-permute-start(bf16[192,1024]{1,0:T(8,128)(2,1)S(1)} %convolution_convert_fusion.2), channel_id=1, source_target_pairs={{0,1},{1,0},{2,3},{3,2},{4,5},{5,4},{6,7},{7,6},{8,9},{9,8},{10,11... | collective-permute-start | bytes 1179656 | tf_op jit(solution)/shard_map/ppermute | solution.py:26
  183.6 36.2 %copy-start.46 = (bf16[1,192,1024]{2,1,0:T(8,128)(2,1)S(1)}, bf16[1,192,1024]{2,1,0:T(8,128)(2,1)}, u32[]{:S(2)}) copy-start(bf16[1,192,1024]{2,1,0:T(8,128)(2,1)} %param.35) | copy-start | bytes 1179652
  226.7 12.3 %collective-permute-start.5 = (bf16[192,1024]{1,0:T(8,128)(2,1)}, bf16[192,1024]{1,0:T(8,128)(2,1)}, u32[]{:S(2)}, u32[]{:S(2)}) collective-permute-start(bf16[192,1024]{1,0:T(8,128)(2,1)} %convolution_convert_fusion), channel_id=1, source_target_pairs={{0,1},{1,0},{2,3},{3,2},{4,5},{5,4},{6,7},{7,6},{8,9},{9,8},{10,11... | collective-permute-start | bytes 1179656 | tf_op jit(solution)/shard_map/ppermute | solution.py:26
  232.8 13.9 %collective-permute-start.4 = (bf16[192,1024]{1,0:T(8,128)(2,1)}, bf16[192,1024]{1,0:T(8,128)(2,1)}, u32[]{:S(2)}, u32[]{:S(2)}) collective-permute-start(bf16[192,1024]{1,0:T(8,128)(2,1)} %convolution_convert_fusion.1), channel_id=1, source_target_pairs={{0,1},{1,0},{2,3},{3,2},{4,5},{5,4},{6,7},{7,6},{8,9},{9,8},{10,11... | collective-permute-start | bytes 1179656 | tf_op jit(solution)/shard_map/ppermute | solution.py:26
  255.3 113.3 %reduce-scatter.12.cloned.1.call-start = ((), (), s32[]{:S(2)}) async-start(), calls=%async_computation.12 | async-start | bytes 2359296 | tf_op jit(solution)/shard_map/reduce_scatter | solution.py:147
  258.8 111.5 %reduce-scatter.16.cloned.1.call-start = ((), (), s32[]{:S(2)}) async-start(), calls=%async_computation.14 | async-start | bytes 3538944
  263.2 162.1 %reduce-scatter.8.cloned.1.call-start = ((), (), s32[]{:S(2)}) async-start(), calls=%async_computation.10 | async-start | bytes 5308416 | tf_op jit(solution)/shard_map/reduce_scatter | solution.py:147
  278.2 9.6 %collective-permute-start.6 = (bf16[4,128,256]{2,1,0:T(8,128)(2,1)S(1)}, bf16[4,128,256]{2,1,0:T(8,128)(2,1)S(1)}, u32[]{:S(2)}, u32[]{:S(2)}) collective-permute-start(bf16[4,128,256]{2,1,0:T(8,128)(2,1)S(1)} %fusion.7), channel_id=1, source_target_pairs={{2,0},{3,1},{6,4},{7,5},{10,8},{11,9},{14,12},{15,13},{18,16},{19,... | collective-permute-start | bytes 786440 | tf_op jit(solution)/shard_map/ppermute | solution.py:19
  308.0 5.9 %collective-permute-start.7 = (f32[3,2048]{1,0:T(4,128)S(1)}, f32[3,2048]{1,0:T(4,128)S(1)}, u32[]{:S(2)}, u32[]{:S(2)}) collective-permute-start(f32[3,2048]{1,0:T(4,128)S(1)} %pad_add_fusion.1), channel_id=1, source_target_pairs={{2,0},{3,1},{6,4},{7,5},{10,8},{11,9},{14,12},{15,13},{18,16},{19,... | collective-permute-start | bytes 73736 | tf_op jit(solution)/shard_map/ppermute | solution.py:19
  321.1 8.9 %collective-permute-start.8 = (bf16[192,1024]{1,0:T(8,128)(2,1)S(1)}, bf16[192,1024]{1,0:T(8,128)(2,1)S(1)}, u32[]{:S(2)}, u32[]{:S(2)}) collective-permute-start(bf16[192,1024]{1,0:T(8,128)(2,1)S(1)} %get-tuple-element.193), channel_id=1, source_target_pairs={{0,1},{1,0},{2,3},{3,2},{4,5},{5,4},{6,7},{7,6},{8,9},{9,8},{10,11... | collective-permute-start | bytes 1179656 | tf_op jit(solution)/shard_map/ppermute | solution.py:26
  334.8 32.2 %copy-start.103 = (f32[192]{0:T(256)S(1)}, f32[192]{0:T(256)}, u32[]{:S(2)}) copy-start(f32[192]{0:T(256)} %copy-done.102) | copy-start | bytes 2308
  334.9 34.3 %copy-start.16 = (f32[192,1024]{1,0:T(8,128)S(1)}, f32[192,1024]{1,0:T(8,128)}, u32[]{:S(2)}) copy-start(f32[192,1024]{1,0:T(8,128)} %copy-done.15) | copy-start | bytes 2359300
  334.9 155.9 %reduce-scatter.14.cloned.1.call-start = ((), (), s32[]{:S(2)}) async-start(), calls=%async_computation.13 | async-start | bytes 6488064 | tf_op jit(solution)/shard_map/reduce_scatter | solution.py:147
  367.1 9.5 %copy-start.57 = (bf16[128,1024]{1,0:T(8,128)(2,1)S(1)}, bf16[128,1024]{1,0:T(8,128)(2,1)}, u32[]{:S(2)}) copy-start(bf16[128,1024]{1,0:T(8,128)(2,1)} %reduce-scatter.10.cloned.1.call-done) | copy-start | bytes 786436
  367.1 9.5 %collective-permute-start.11 = (bf16[128,1024]{1,0:T(8,128)(2,1)}, bf16[128,1024]{1,0:T(8,128)(2,1)S(1)}, u32[]{:S(2)}, u32[]{:S(2)}) collective-permute-start(bf16[128,1024]{1,0:T(8,128)(2,1)} %reduce-scatter.10.cloned.1.call-done), channel_id=1, source_target_pairs={{0,2},{2,0},{1,3},{3,1},{4,6},{6,4},{5,7},{7,5},{8,10},{10,8},{9,1... | collective-permute-start | bytes 786440 | tf_op jit(solution)/shard_map/ppermute | solution.py:26
  368.6 58.2 %collective-permute-start.12 = (bf16[128,1024]{1,0:T(8,128)(2,1)}, bf16[128,1024]{1,0:T(8,128)(2,1)S(1)}, u32[]{:S(2)}, u32[]{:S(2)}) collective-permute-start(bf16[128,1024]{1,0:T(8,128)(2,1)} %reduce-scatter.12.cloned.1.call-done), channel_id=1, source_target_pairs={{0,2},{2,0},{1,3},{3,1},{4,6},{6,4},{5,7},{7,5},{8,10},{10,8},{9,1... | collective-permute-start | bytes 786440 | tf_op jit(solution)/shard_map/ppermute | solution.py:26
  370.3 56.5 %copy-start.56 = (bf16[128,1024]{1,0:T(8,128)(2,1)S(1)}, bf16[128,1024]{1,0:T(8,128)(2,1)}, u32[]{:S(2)}) copy-start(bf16[128,1024]{1,0:T(8,128)(2,1)} %reduce-scatter.12.cloned.1.call-done) | copy-start | bytes 786436
  371.6 56.1 %collective-permute-start.14 = (bf16[128,1536]{0,1:T(8,128)(2,1)S(1)}, bf16[128,1536]{0,1:T(8,128)(2,1)S(1)}, u32[]{:S(2)}, u32[]{:S(2)}) collective-permute-start(bf16[128,1536]{0,1:T(8,128)(2,1)S(1)} %copy.391), channel_id=1, source_target_pairs={{0,2},{2,0},{1,3},{3,1},{4,6},{6,4},{5,7},{7,5},{8,10},{10,8},{9,1... | collective-permute-start | bytes 1179656 | tf_op jit(solution)/shard_map/ppermute | solution.py:26
  425.3 13.4 %collective-permute-start.9 = (bf16[128,2304]{1,0:T(8,128)(2,1)}, bf16[128,2304]{1,0:T(8,128)(2,1)S(1)}, u32[]{:S(2)}, u32[]{:S(2)}) collective-permute-start(bf16[128,2304]{1,0:T(8,128)(2,1)} %reduce-scatter.8.cloned.1.call-done), channel_id=1, source_target_pairs={{0,2},{2,0},{1,3},{3,1},{4,6},{6,4},{5,7},{7,5},{8,10},{10,8},{9,1... | collective-permute-start | bytes 1769480 | tf_op jit(solution)/shard_map/ppermute | solution.py:26
  427.6 11.1 %copy-start.53 = (bf16[128,2304]{1,0:T(8,128)(2,1)S(1)}, bf16[128,2304]{1,0:T(8,128)(2,1)}, u32[]{:S(2)}) copy-start(bf16[128,2304]{1,0:T(8,128)(2,1)} %reduce-scatter.8.cloned.1.call-done) | copy-start | bytes 1769476
  438.9 57.1 %collective-permute-start.10 = (bf16[128,3]{1,0:T(8,128)(2,1)S(1)}, bf16[128,3]{1,0:T(8,128)(2,1)S(1)}, u32[]{:S(2)}, u32[]{:S(2)}) collective-permute-start(bf16[128,3]{1,0:T(8,128)(2,1)S(1)} %slice.310), channel_id=1, source_target_pairs={{0,1},{1,0},{2,3},{3,2},{4,5},{5,4},{6,7},{7,6},{8,9},{9,8},{10,11... | collective-permute-start | bytes 2312 | tf_op jit(solution)/shard_map/ppermute | solution.py:26
  490.7 16.2 %copy-start.52 = (bf16[128,2816]{1,0:T(8,128)(2,1)S(1)}, bf16[128,2816]{1,0:T(8,128)(2,1)}, u32[]{:S(2)}) copy-start(bf16[128,2816]{1,0:T(8,128)(2,1)} %reduce-scatter.14.cloned.1.call-done) | copy-start | bytes 2162692
  490.7 16.2 %collective-permute-start.13 = (bf16[128,2816]{1,0:T(8,128)(2,1)}, bf16[128,2816]{1,0:T(8,128)(2,1)S(1)}, u32[]{:S(2)}, u32[]{:S(2)}) collective-permute-start(bf16[128,2816]{1,0:T(8,128)(2,1)} %reduce-scatter.14.cloned.1.call-done), channel_id=1, source_target_pairs={{0,2},{2,0},{1,3},{3,1},{4,6},{6,4},{5,7},{7,5},{8,10},{10,8},{9,1... | collective-permute-start | bytes 2162696 | tf_op jit(solution)/shard_map/ppermute | solution.py:26
  (100 other events, 336.3 us)
Sparse Core Ops, SparseCore 0:
  9.6 31.9 all-gather.7
  43.8 48.3 all-gather.5
  93.8 28.0 all-gather.9
  123.9 59.6 all-gather.11
  185.1 34.6 all-gather.13
  255.4 35.1 reduce-scatter.9
  292.9 34.5 reduce-scatter.11
  329.8 39.1 reduce-scatter.15
  371.3 53.9 reduce-scatter.7
  427.5 63.2 reduce-scatter.13
